TPU v7x, 128 devices: a whole 4x4x4 slice. The times are simulated.
128 devices in a mesh: src: 16 (over y_lo, z, core), rcv: 8 (over x, y_hi).
Axes of the slice: x: 4, y: 4 (y_hi: 2, y_lo: 2; y = y_hi * 2 + y_lo), z: 4, core: 2. Of those that a mesh axis runs over, the one named last changes fastest.
Arguments:
- traces: float32 [1024, 1024, 512], P(('src', 'rcv')), may hold values from -6 to 6
- sketch: float32 [1024, 64], replicated, may hold values from -0.1875 to 0.1875
Outputs:
- range_basis: float32 [32, 2, 1024, 64], P('rcv', None, 'src')
- r_factor: float32 [32, 64, 64], P('rcv')
All inputs are finite; a program needn't handle non-finite values.
Results may differ from a plain program's by a relative error of at most 0.0003.
Values sent between devices are 32-bit elements; how exact they have to be, the bound alone decides.
No kernel may reach another device: no remote copies, remote signals or barrier semaphores. Data moves between devices by JAX's collectives and lax.ppermute only.
A program may use at most 128 MiB of HBM per device.

v0:
```python
import math

import jax
import jax.numpy as jnp
from jax import lax
from jax.sharding import PartitionSpec as P

FREQS = 32
RANK = 64


def dft_rows(samples):
    time_index = jnp.arange(samples, dtype=jnp.int32)
    orders = jnp.arange(1, FREQS + 1, dtype=jnp.int32)
    phases = orders[:, None] * time_index[None, :] % samples
    angles = phases.astype(jnp.float32) * (2.0 * math.pi / samples)
    weights = jnp.stack([jnp.cos(angles), -jnp.sin(angles)], axis=1)
    return weights.reshape(2 * FREQS, samples) * (1.0 / math.sqrt(samples))


def gram_of(stacked):
    return jnp.einsum("fkr,flr->fkl", stacked, stacked, precision=lax.Precision.HIGHEST)


def local(traces, sketch):
    shot_count, receivers, samples = traces.shape
    src_count = lax.axis_size("src")
    rcv_count = lax.axis_size("rcv")
    local_freqs = FREQS // rcv_count
    tile_rows = receivers // src_count
    spectrum = lax.dot_general(
        dft_rows(samples),
        traces.reshape(shot_count * receivers, samples),
        (((1,), (1,)), ((), ())),
        precision=lax.Precision.HIGHEST,
    )
    spectrum = spectrum.reshape(FREQS, 2, shot_count, receivers)
    own_sketched = jnp.einsum("fpin,nk->fpik", spectrum, sketch, precision=lax.Precision.HIGHEST)
    direct = lax.all_to_all(own_sketched, "rcv", split_axis=0, concat_axis=2, tiled=True)
    blocks = spectrum.reshape(rcv_count, local_freqs, 2, shot_count, src_count, tile_rows)
    blocks = jnp.transpose(blocks, (4, 0, 1, 2, 3, 5)).reshape(
        src_count * rcv_count, local_freqs, 2, shot_count, tile_rows
    )
    received = lax.all_to_all(blocks, ("src", "rcv"), split_axis=0, concat_axis=0, tiled=True)
    sketch_blocks = sketch.reshape(src_count * rcv_count, shot_count, RANK)
    reverse = jnp.einsum(
        "dfpir,dik->fprk", received, sketch_blocks, precision=lax.Precision.HIGHEST
    )
    sketched = 0.5 * (direct + reverse)
    stacked = jnp.swapaxes(sketched.reshape(local_freqs, 2 * tile_rows, RANK), 1, 2)
    gram_one = lax.psum(gram_of(stacked), "src")
    lower_one = jnp.linalg.cholesky(gram_one)
    orthonormal = jax.scipy.linalg.solve_triangular(lower_one, stacked, lower=True)
    scaling = math.sqrt(2.0 * receivers)
    range_basis = jnp.swapaxes(orthonormal, 1, 2).reshape(local_freqs, 2, tile_rows, RANK) * scaling
    r_factor = jnp.swapaxes(lower_one, 1, 2) / scaling
    return (range_basis, r_factor)


def solution(mesh):
    in_specs = (P(("src", "rcv"), None, None), P())
    out_specs = (P("rcv", None, "src", None), P("rcv", None, None))
    return jax.shard_map(local, mesh=mesh, in_specs=in_specs, out_specs=out_specs, check_vma=False)
```

profile of v0, /device:TPU:0, one launch (start us, length us, event | category | flops | bytes accessed | tf_op | source)
XLA Modules:
  0.0 283.5 jit_solution(8640894344110395717)
XLA Ops:
  7.2 0.3 fusion.22
  7.5 0.1 copy.67
  7.7 0.1 mul.86
  7.8 19.3 %fusion.23 = f32[64,8192]{1,0:T(8,128)S(1)} fusion(f32[64,512]{1,0:T(8,128)S(1)} %mul.86, f32[8192,512]{1,0:T(8,128)} %bitcast.46), kind=kOutput, calls=%fused_computation.32 | convolution fusion | flops 3221225472 | bytes 19005440 | tf_op jit(solution)/shard_map/dot_general | solution.py:31
  27.1 0.0 copy-start
  27.1 1.2 copy.92
  28.3 0.0 copy-done
  28.3 1.8 fusion.12
  30.1 0.8 reshape.151
  30.9 7.0 %all-to-all-start = ((f32[8,1,4096]{2,1,0:T(1,128)}), f32[8,1,4096]{2,1,0:T(1,128)S(1)}, u32[]{:S(2)}, u32[]{:S(2)}) async-start(f32[8,1,4096]{2,1,0:T(1,128)} %reshape.151), calls=%async_computation | async-start | bytes 262144 | tf_op jit(solution)/shard_map/all_to_all | solution.py:39
  38.0 3.0 %reshape_reshape.3 = f32[8,4,2,8,16,64]{5,4,3,2,1,0:T(8,128)} reshape(f32[64,8192]{1,0:T(8,128)S(1)} %fusion.23) | data formatting | bytes 4194304 | tf_op jit(solution)/shard_map/reshape;reshape | solution.py:40
  41.0 5.5 %copy.69 = f32[8,4,2,8,16,64]{5,3,2,1,0,4:T(8,128)} copy(f32[8,4,2,8,16,64]{5,4,3,2,1,0:T(8,128)} %reshape_reshape.3) | data formatting | bytes 4194304 | tf_op jit(solution)/shard_map/reshape;reshape | solution.py:40
  46.5 5.6 %reshape.149 = f32[128,1,4096]{2,1,0:T(1,128)} reshape(f32[128,4,2,8,64]{4,3,2,1,0:T(8,128)} %bitcast.48) | data formatting | bytes 4194304
  52.1 0.0 all-to-all-done
  52.1 11.9 %all-to-all-start.1 = ((f32[128,1,4096]{2,1,0:T(1,128)}), f32[128,1,4096]{2,1,0:T(1,128)}, u32[]{:S(2)}, u32[]{:S(2)}) async-start(f32[128,1,4096]{2,1,0:T(1,128)} %reshape.149), calls=%async_computation.1 | async-start | bytes 4194304 | tf_op jit(solution)/shard_map/all_to_all | solution.py:44
  63.9 0.0 all-reduce.2.cloned.1.call-start
  64.0 0.2 copy.70
  64.2 0.5 broadcast.178
  64.7 1.0 reduce.7
  65.7 0.1 reshape.152
  65.8 27.0 %all-to-all-done.1 = f32[128,1,4096]{2,1,0:T(1,128)} async-done(((f32[128,1,4096]{2,1,0:T(1,128)}), f32[128,1,4096]{2,1,0:T(1,128)}, u32[]{:S(2)}, u32[]{:S(2)}) %all-to-all-start.1) | async-done | bytes 2097184 | tf_op jit(solution)/shard_map/all_to_all | solution.py:44
  92.8 7.3 %reduce.6 = f32[128,4096]{1,0:T(8,128)S(1)} reduce(f32[128,1,4096]{2,1,0:T(1,128)} %all-to-all-done.1, f32[]{:T(128)} %broadcast.178), dimensions={1}, to_apply=%all_to_all.20.reduce_sub_computation | reduce | bytes 4194308 | tf_op jit(solution)/shard_map/all_to_all | solution.py:44
  100.1 3.2 %reshape.150 = f32[128,4,2,8,64]{4,3,2,1,0:T(8,128)} reshape(f32[128,4096]{1,0:T(8,128)S(1)} %reduce.6) | data formatting | bytes 4194304
  103.3 10.5 %fusion.8 = f32[4,2,64,64]{3,2,1,0:T(8,128)S(1)} fusion(f32[128,4,2,8,64]{4,3,2,1,0:T(8,128)} %reshape.150, f32[128,8,64,1,1]{2,1,0,4,3:T(8,128)S(1)} %bitcast.52, f32[4,2,8,8,64]{4,3,1,0,2:T(8,128)S(1)} %bitcast.53), kind=kOutput, calls=%fused_computation.4 | convolution fusion | flops 402718720 | bytes 2621440 | tf_op jit(solution)/shard_map/dfpir,dik->fprk/dot_general | solution.py:46
  113.8 1.2 fusion.24
  115.1 0.0 all-reduce.2.cloned.1.call-update
  115.1 114.0 %all-reduce.2.cloned.1.call-done = f32[4,64,64]{1,2,0:T(8,128)} async-done(((f32[4,64,64]{1,2,0:T(8,128)}), f32[4,64,64]{1,2,0:T(8,128)}) %all-reduce.2.cloned.1.call-update) | async-done | bytes 65552 | tf_op jit(solution)/shard_map/psum | solution.py:51
  229.1 1.0 copy.76
  230.1 0.9 fusion.15
  231.1 23.5 %custom-call.8 = f32[4,64,64]{2,1,0:T(8,128)S(1)} custom-call(f32[4,64,64]{2,1,0:T(8,128)S(1)} %fusion.15), custom_call_target="Cholesky" | custom-call | tf_op jit(solution)/shard_map/jit(cholesky)/cholesky | solution.py:52
  254.6 0.1 compare_reduce_fusion
  254.7 0.1 multiply_bitcast_fusion
  254.8 0.8 copy.80
  255.5 19.6 %custom-call.9 = f32[4,1,64,64]{2,3,1,0:T(8,128)S(1)} custom-call(f32[4,1,64,64]{3,2,1,0:T(8,128)S(1)} %get-tuple-element.15), custom_call_target="InvertDiagBlocksLowerTriangular" | custom-call | tf_op jit(solution)/shard_map/jit(_solve_triangular)/vmap()/triangular_solve | solution.py:53
  275.2 0.7 convolution_multiply_fusion
  275.9 0.8 copy.91
  (5 shorter events, 0.1 us)
Async XLA Ops:
  27.1 1.2 copy-start
  30.9 21.1 %all-to-all-start = ((f32[8,1,4096]{2,1,0:T(1,128)}), f32[8,1,4096]{2,1,0:T(1,128)S(1)}, u32[]{:S(2)}, u32[]{:S(2)}) async-start(f32[8,1,4096]{2,1,0:T(1,128)} %reshape.151), calls=%async_computation | async-start | bytes 262144 | tf_op jit(solution)/shard_map/all_to_all | solution.py:39
  52.1 40.7 %all-to-all-start.1 = ((f32[128,1,4096]{2,1,0:T(1,128)}), f32[128,1,4096]{2,1,0:T(1,128)}, u32[]{:S(2)}, u32[]{:S(2)}) async-start(f32[128,1,4096]{2,1,0:T(1,128)} %reshape.149), calls=%async_computation.1 | async-start | bytes 4194304 | tf_op jit(solution)/shard_map/all_to_all | solution.py:44
  63.9 165.2 %all-reduce.2.cloned.1.call-start = ((), (), s32[]{:S(2)}) async-start(), calls=%async_computation.2 | async-start | bytes 262144 | tf_op jit(solution)/shard_map/psum | solution.py:51
Sparse Core Ops, SparseCore 0:
  115.2 113.8 all-reduce.1
where the time goes:
time: 285 us; the launch traced here: 284 us
  waiting for transfers between devices  141 us (49%)
  other arithmetic  52.9 us (19%)
  matrix products  33.5 us (12%)
  local copies, waits for them, and re-layouts  22.9 us (8%)
  starting transfers between devices  18.9 us (7%)
  between operations  14.2 us (5%)
    psum x1, waiting for transfers between devices, local(): gram_one = lax.psum(gram_of(stacked), 'src')  114 us
    all_to_all x1, waiting for transfers between devices, local(): lax.all_to_all(blocks, ('src', 'rcv'), split_axis=0, concat_axis=0, tiled...  27 us
    another operation x4, other arithmetic, local(): lower_one = jnp.linalg.cholesky(gram_one)  23.6 us
    another operation x2, other arithmetic, local(): jax.scipy.linalg.solve_triangular(lower_one, stacked, lower=True)  19.7 us
    dot_general x1, matrix products, local(): lax.dot_general(dft_rows(samples), traces.reshape(shot_count * receivers,...  19.3 us
    unnamed x10, local copies, waits for them, and re-layouts  12.7 us
    all_to_all x1, starting transfers between devices, local(): lax.all_to_all(blocks, ('src', 'rcv'), split_axis=0, concat_axis=0, tiled...  11.9 us
    dot_general x1, matrix products, local(): jnp.einsum('dfpir,dik->fprk', received, sketch_blocks, precision=lax.Prec...  10.5 us
  transfers between devices with their start and end apart: 3, of which 2 were waited for; matrix products, arithmetic and copies ran while one was open for 6% of the time, Pallas kernels for 0%

commit v1 on v0

v1 whole, which is shorter than its diff:
```python
import math

import jax
import jax.numpy as jnp
import numpy as np
from jax import lax
from jax.experimental import pallas as pl
from jax.experimental.pallas import tpu as pltpu
from jax.sharding import PartitionSpec as P

FREQS = 32
RANK = 64
F32 = jnp.float32
BF16 = jnp.bfloat16
NT = (((1,), (1,)), ((), ()))
NN = (((1,), (0,)), ((), ()))


def dft_rows(samples):
    times = np.arange(samples)
    orders = np.arange(1, FREQS + 1)
    angles = (orders[:, None] * times[None, :] % samples) * (2.0 * math.pi / samples)
    weights = np.stack([np.cos(angles), -np.sin(angles)], axis=1)
    return (weights.reshape(2 * FREQS, samples) / math.sqrt(samples)).astype(np.float32)


def split(x):
    high = x.astype(BF16)
    return high, (x - high.astype(F32)).astype(BF16)


def mm(a, b, dims):
    return lax.dot_general(a, b, dims, preferred_element_type=F32)


def low_lanes(shape):
    return lax.broadcasted_iota(jnp.int32, shape, 1) < 64


def dft_kernel(x_ref, w_ref, st_ref, spec_ref, d_ref):
    weights = w_ref[...]
    parts = [[None, None] for _ in range(4)]
    for tile in range(2):
        for half in range(2):
            x = x_ref[4 * half : 4 * half + 4, 64 * tile : 64 * tile + 64, :].reshape(256, -1)
            high, low = split(x)
            both = mm(weights, high, NT)
            out = both[:64] + both[64:] + mm(weights[:64], low, NT)
            for c in range(2):
                piece = out[:, 128 * c : 128 * c + 128]
                spec_ref[8 * tile : 8 * tile + 8, 2 * half + c] = piece.reshape(8, 8, 128)
                parts[2 * half + c][tile] = piece
    rows = jnp.concatenate([jnp.concatenate(p, axis=1) for p in parts], axis=0)
    st = st_ref[...]
    rolled = pltpu.roll(st, 64, 1)
    low_half = low_lanes(st.shape)
    zero = jnp.zeros_like(st)
    even = jnp.concatenate([jnp.where(low_half, st, zero), jnp.where(low_half, rolled, zero)], axis=1)
    odd = jnp.concatenate([jnp.where(low_half, zero, rolled), jnp.where(low_half, zero, st)], axis=1)
    s_high, s_low = split(jnp.concatenate([even, odd], axis=0))
    high, low = split(rows)
    both = mm(high, jnp.concatenate([s_high, s_low], axis=0), NT)
    out = both[:, :128] + both[:, 128:] + mm(low, s_high, NT)

    @pl.when(pl.program_id(0) == 0)
    def _():
        d_ref[...] = jnp.zeros_like(d_ref)

    for a in range(4):
        d_ref[:, a] += out[64 * a : 64 * a + 64].reshape(8, 8, 128)


def sketch_kernel(r_ref, d_ref, s_ref, gram_ref, z_ref, dn_ref):
    depth = r_ref.shape[0] // 8
    s_even = s_ref[pl.ds(0, depth, stride=2), :]
    s_odd = s_ref[pl.ds(1, depth, stride=2), :]
    s_high, s_low = split(jnp.transpose(jnp.concatenate([s_even, s_odd], axis=1)))
    s_both = jnp.concatenate([s_high, s_low], axis=0)
    low_half = low_lanes((64, 128))
    low_rows = low_lanes((32, 128))
    for q in range(2):
        halves = []
        for f in range(2):
            sums = []
            for p in range(2):
                part = 4 * q + 2 * f + p
                high, low = split(r_ref[pl.ds(part, depth, stride=8), :])
                both = mm(s_both, high, NN)
                sums.append(both[:128] + both[128:] + mm(s_high, low, NN))
            x, y = sums
            halves.append(
                jnp.where(
                    low_half,
                    x[:64] + pltpu.roll(x[64:], 64, 1),
                    pltpu.roll(y[:64], 64, 1) + y[64:],
                )
            )
        reverse = jnp.transpose(jnp.concatenate(halves, axis=0))
        for p in range(2):
            first = d_ref[pl.ds(4 * q + p, 32, stride=8), :]
            second = d_ref[pl.ds(4 * q + 2 + p, 32, stride=8), :]
            dn_ref[pl.ds(64 * p, 32, stride=2), :] = jnp.where(low_rows, first, pltpu.roll(second, 64, 1))
            dn_ref[pl.ds(64 * p + 1, 32, stride=2), :] = jnp.where(low_rows, pltpu.roll(first, 64, 1), second)
        z = 0.5 * (dn_ref[...] + reverse)
        z_ref[q] = z
        gram = lax.dot_general(z, z, (((0,), (0,)), ((), ())), precision=lax.Precision.HIGHEST, preferred_element_type=F32)
        gram_ref[q] = jnp.where(low_half, gram[:64], gram[64:])


def factor_kernel(scaling, g_ref, h_ref, z_ref, basis_ref, r_ref, u_ref, l_ref):
    lane = lax.broadcasted_iota(jnp.int32, (8, 128), 1)
    sub = lax.broadcasted_iota(jnp.int32, (8, 128), 0)
    base = lane - lane % 64
    inner = lane % 64
    g = [[g_ref[q, 8 * b : 8 * b + 8, :] + h_ref[q, 8 * b : 8 * b + 8, :] for b in range(8)] for q in range(2)]
    e = [[jnp.where(inner == sub + 8 * b, 1.0, 0.0).astype(F32) for b in range(8)] for q in range(2)]
    for j in range(64):
        top, row = j // 8, j % 8
        index = base + j
        for q in range(2):
            cols = {b: jnp.take_along_axis(g[q][b], index, axis=1) for b in range(top, 8)}
            pivot = jnp.broadcast_to(cols[top][row : row + 1], (8, 128))
            grow = jnp.broadcast_to(g[q][top][row : row + 1], (8, 128))
            erow = jnp.broadcast_to(e[q][top][row : row + 1], (8, 128))
            scale = lax.rsqrt(pivot)
            scale = scale * (1.5 - 0.5 * pivot * scale * scale)
            u_ref[q, j : j + 1, :] = jnp.where(inner >= j, grow * scale, 0.0)[:1]
            l_ref[q, j : j + 1, :] = (erow * scale)[:1]
            inverse = 1.0 / pivot
            grow = grow * inverse
            erow = erow * inverse
            for b in range(top, 8):
                c = cols[b]
                if b == top:
                    c = jnp.where(sub > row, c, 0.0)
                g[q][b] = g[q][b] - c * grow
                e[q][b] = e[q][b] - c * erow
    low_half = low_lanes((64, 128))
    for q in range(2):
        u = u_ref[q] * (1.0 / scaling)
        r_ref[2 * q] = u[:, :64]
        r_ref[2 * q + 1] = pltpu.roll(u, 64, 1)[:, :64]
        inv = l_ref[q]
        inv = jnp.concatenate([jnp.where(low_half, inv, 0.0), jnp.where(low_half, 0.0, inv)], axis=0)
        out = lax.dot_general(z_ref[q], inv, NT, precision=lax.Precision.HIGHEST, preferred_element_type=F32) * scaling
        turned = pltpu.roll(out, 64, 1)
        for p in range(2):
            basis_ref[2 * q, p] = out[64 * p : 64 * p + 64, :64]
            basis_ref[2 * q + 1, p] = turned[64 * p : 64 * p + 64, :64]


def local(traces, sketch):
    shots, receivers, samples = traces.shape
    devices = lax.axis_size("src") * lax.axis_size("rcv")
    rcv_count = lax.axis_size("rcv")
    weights = dft_rows(samples)
    w_high = weights.astype(BF16)
    w_low = (weights - w_high.astype(np.float32)).astype(BF16)
    w_both = jnp.asarray(np.concatenate([w_high, w_low], axis=0))
    sd = jax.ShapeDtypeStruct
    spec, own = pl.pallas_call(
        dft_kernel,
        grid=(receivers // 128,),
        in_specs=[
            pl.BlockSpec((shots, 128, samples), lambda g: (0, g, 0)),
            pl.BlockSpec((128, samples), lambda g: (0, 0)),
            pl.BlockSpec((RANK, 128), lambda g: (0, g)),
        ],
        out_specs=[
            pl.BlockSpec((16, 4, 8, 128), lambda g: (g, 0, 0, 0)),
            pl.BlockSpec((rcv_count, 4, 8, 128), lambda g: (0, 0, 0, 0)),
        ],
        out_shape=[sd((devices, 4, 8, 128), F32), sd((rcv_count, 4, 8, 128), F32)],
        name="dft",
    )(traces, w_both, sketch.T)
    direct = lax.all_to_all(own.reshape(rcv_count, 32, 128), "rcv", split_axis=0, concat_axis=0, tiled=True)
    received = lax.all_to_all(spec.reshape(devices, 32, 128), ("src", "rcv"), split_axis=0, concat_axis=0, tiled=True)
    gram, z = pl.pallas_call(
        sketch_kernel,
        out_shape=[sd((2, 64, 128), F32), sd((2, 128, 128), F32)],
        scratch_shapes=[pltpu.VMEM((128, 128), F32)],
        name="sketch",
    )(received.reshape(devices * 32, 128), direct.reshape(rcv_count * 32, 128), sketch)
    src = lax.axis_size("src")
    for bits in (1, 8, 2):
        gram = gram + lax.ppermute(gram, "src", [(s, s ^ bits) for s in range(src)])
    other = lax.ppermute(gram, "src", [(s, s ^ 6) for s in range(src)])
    scaling = math.sqrt(2.0 * receivers)
    basis, r_factor = pl.pallas_call(
        lambda *refs: factor_kernel(scaling, *refs),
        out_shape=[sd((4, 2, 64, 64), F32), sd((4, 64, 64), F32)],
        scratch_shapes=[pltpu.VMEM((2, 64, 128), F32), pltpu.VMEM((2, 64, 128), F32)],
        name="factor",
    )(gram, other, z)
    return basis, r_factor


def solution(mesh):
    in_specs = (P(("src", "rcv"), None, None), P())
    out_specs = (P("rcv", None, "src", None), P("rcv", None, None))
    return jax.shard_map(local, mesh=mesh, in_specs=in_specs, out_specs=out_specs, check_vma=False)
```

time: 285 us -> 95.9 us (0.34)
  waiting for transfers between devices: 141 us -> 42.1 us
  other arithmetic: 52.9 us -> 0.87 us
  matrix products: 33.5 us -> 0 us
  Pallas kernels: 0 us -> 24.8 us
  local copies, waits for them, and re-layouts: 22.9 us -> 2.95 us
  blocking collectives: 0 us -> 15.1 us
  between operations: 14.2 us -> 0.67 us
  starting transfers between devices: 18.9 us -> 8.97 us
    psum x1 -> x0, waiting for transfers between devices: 114 us -> none  [local(): gram_one = lax.psum(gram_of(stacked), 'src')]
    another operation x6 -> x0, other arithmetic: 43.3 us -> none  [the longest x4 23.6 us: local(): lower_one = jnp.linalg.cholesky(gram_one)]
    dot_general x4 -> x0, matrix products: 32.8 us -> none  [the longest x1 19.3 us: local(): lax.dot_general(dft_rows(samples), traces.reshape(shot_count * receivers,...]
    pallas_call x0 -> x3, Pallas kernels: none -> 24.8 us  [the longest x1 12.8 us: local(): pl.pallas_call(dft_kernel, grid=(receivers // 128,), in_specs=[pl.BlockSp...]
    all_to_all x0 -> x1, blocking collectives: none -> 15.1 us  [local(): lax.all_to_all(own.reshape(rcv_count, 32, 128), 'rcv', split_axis=0, conc...]
    ppermute x0 -> x4, waiting for transfers between devices: none -> 13.8 us  [the longest x3 9.1 us: local(): gram = gram + lax.ppermute(gram, 'src', [(s, s ^ bits) for s in range(src)])]
    all_to_all x2 -> x1, starting transfers between devices: 18.9 us -> 7.04 us  [local(): lax.all_to_all(spec.reshape(devices, 32, 128), ('src', 'rcv'), split_axis...]
    unnamed x10 -> x9, local copies, waits for them, and re-layouts: 12.7 us -> 2.95 us
  transfers between devices with their start and end apart: 3 -> 5, of which waited for: 2 -> 5; matrix products, arithmetic and copies ran while one was open for 6% -> 1% of each run, Pallas kernels for 0% -> 0%
where the time goes in v1:
time: 95.9 us; the launch traced here: 95.4 us
  waiting for transfers between devices  42.1 us (44%)
  Pallas kernels  24.8 us (26%)
  blocking collectives  15.1 us (16%)
  starting transfers between devices  8.97 us (9%)
  local copies, waits for them, and re-layouts  2.95 us (3%)
    all_to_all x1, waiting for transfers between devices, local(): lax.all_to_all(spec.reshape(devices, 32, 128), ('src', 'rcv'), split_axis...  28.3 us
    all_to_all x1, blocking collectives, local(): lax.all_to_all(own.reshape(rcv_count, 32, 128), 'rcv', split_axis=0, conc...  15.1 us
    pallas_call x1, Pallas kernels, local(): pl.pallas_call(dft_kernel, grid=(receivers // 128,), in_specs=[pl.BlockSp...  12.8 us
    ppermute x3, waiting for transfers between devices, local(): gram = gram + lax.ppermute(gram, 'src', [(s, s ^ bits) for s in range(src)])  9.1 us
    pallas_call x1, Pallas kernels, local(): pl.pallas_call(lambda *refs: factor_kernel(scaling, *refs), out_shape=[sd...  7.49 us
    all_to_all x1, starting transfers between devices, local(): lax.all_to_all(spec.reshape(devices, 32, 128), ('src', 'rcv'), split_axis...  7.04 us
    ppermute x1, waiting for transfers between devices, local(): other = lax.ppermute(gram, 'src', [(s, s ^ 6) for s in range(src)])  4.67 us
    pallas_call x1, Pallas kernels, local(): pl.pallas_call(sketch_kernel, out_shape=[sd((2, 64, 128), F32), sd((2, 12...  4.49 us
  transfers between devices with their start and end apart: 5, of which 5 were waited for; matrix products, arithmetic and copies ran while one was open for 1% of the time, Pallas kernels for 0%

profile of v1, /device:TPU:0, one launch (start us, length us, event | category | flops | bytes accessed | tf_op | source)
XLA Modules:
  0.0 95.4 jit_solution(10875056303451397138)
XLA Ops:
  0.6 12.8 %dft.1 = (f32[128,4,8,128]{3,2,1,0:T(8,128)}, f32[8,4,8,128]{3,2,1,0:T(8,128)}) custom-call(f32[8,1024,512]{2,1,0:T(8,128)} %x_ref.1, bf16[128,512]{1,0:T(8,128)(2,1)} %constant.2.clone.w_ref, f32[64,1024]{1,0:T(8,128)} %bitcast.7), custom_call_target="tpu_custom_call" | custom-call | tf_op jit(solution)/shard_map/dft/pallas_call | solution.py:161
  13.4 15.1 %all_to_all.10 = f32[8,32,128]{2,1,0:T(8,128)} all-to-all(f32[8,32,128]{2,1,0:T(8,128)} %bitcast.9), channel_id=1, replica_groups=mesh['src'=16,'rcv'=8] {'rcv'}, dimensions={0} | all-to-all | bytes 262144 | tf_op jit(solution)/shard_map/all_to_all | solution.py:176
  28.5 0.0 copy-start.1
  28.5 7.0 %all-to-all-start = ((f32[128,32,128]{2,1,0:T(8,128)}), f32[128,32,128]{2,1,0:T(8,128)S(1)}, u32[]{:S(2)}, u32[]{:S(2)}) async-start(f32[128,32,128]{2,1,0:T(8,128)} %bitcast.6), calls=%async_computation | async-start | bytes 4194304 | tf_op jit(solution)/shard_map/all_to_all | solution.py:177
  35.5 0.0 copy-done.1
  35.6 1.0 %copy.5.s_ref = f32[1024,64]{1,0:T(8,128)} copy(f32[1024,64]{0,1:T(8,128)S(1)} %copy-done.1) | data formatting | bytes 524288 | tf_op args[1]
  36.6 28.3 %all-to-all-done = f32[128,32,128]{2,1,0:T(8,128)S(1)} async-done(((f32[128,32,128]{2,1,0:T(8,128)}), f32[128,32,128]{2,1,0:T(8,128)S(1)}, u32[]{:S(2)}, u32[]{:S(2)}) %all-to-all-start) | async-done | bytes 2097184 | tf_op jit(solution)/shard_map/all_to_all | solution.py:177
  64.9 0.0 copy-start
  64.9 1.3 %copy-done = f32[128,32,128]{2,1,0:T(8,128)} copy-done((f32[128,32,128]{2,1,0:T(8,128)}, f32[128,32,128]{2,1,0:T(8,128)S(1)}, u32[]{:S(2)}) %copy-start) | copy-done | bytes 2097176
  66.2 4.5 %sketch.1 = (f32[2,64,128]{2,1,0:T(8,128)}, f32[2,128,128]{2,1,0:T(8,128)}) custom-call(f32[4096,128]{1,0:T(8,128)} %bitcast.5, f32[256,128]{1,0:T(8,128)} %bitcast.8, f32[1024,64]{1,0:T(8,128)} %copy.5.s_ref), custom_call_target="tpu_custom_call" | custom-call | tf_op jit(solution)/shard_map/sketch/pallas_call | solution.py:178
  70.7 0.0 collective-permute-start
  70.7 1.5 %collective-permute-done = f32[2,64,128]{2,1,0:T(8,128)S(1)} collective-permute-done((f32[2,64,128]{2,1,0:T(8,128)}, f32[2,64,128]{2,1,0:T(8,128)S(1)}, u32[]{:S(2)}, u32[]{:S(2)}) %collective-permute-start) | collective-permute-done | bytes 65568 | tf_op jit(solution)/shard_map/ppermute | solution.py:186
  72.1 0.9 add.9
  73.0 0.7 collective-permute-start.1
  73.7 3.6 %collective-permute-done.1 = f32[2,64,128]{2,1,0:T(8,128)S(1)} collective-permute-done((f32[2,64,128]{2,1,0:T(8,128)S(1)}, f32[2,64,128]{2,1,0:T(8,128)S(1)}, u32[]{:S(2)}, u32[]{:S(2)}) %collective-permute-start.1) | collective-permute-done | bytes 65568 | tf_op jit(solution)/shard_map/ppermute | solution.py:186
  77.3 0.3 collective-permute-start.2
  77.7 4.0 %collective-permute-done.2 = f32[2,64,128]{2,1,0:T(8,128)S(1)} collective-permute-done((f32[2,64,128]{2,1,0:T(8,128)S(1)}, f32[2,64,128]{2,1,0:T(8,128)S(1)}, u32[]{:S(2)}, u32[]{:S(2)}) %collective-permute-start.2) | collective-permute-done | bytes 65568 | tf_op jit(solution)/shard_map/ppermute | solution.py:186
  81.7 0.0 copy-start.2
  81.7 0.9 collective-permute-start.3
  82.6 4.7 %collective-permute-done.3.refs_1_ = f32[2,64,128]{2,1,0:T(8,128)S(1)} collective-permute-done((f32[2,64,128]{2,1,0:T(8,128)S(1)}, f32[2,64,128]{2,1,0:T(8,128)S(1)}, u32[]{:S(2)}, u32[]{:S(2)}) %collective-permute-start.3) | collective-permute-done | bytes 65568 | tf_op jit(solution)/shard_map/ppermute | solution.py:187
  87.3 0.0 copy-start.3
  87.3 0.0 copy-done.2
  87.3 0.6 copy-done.3
  87.9 7.5 %factor.1 = (f32[4,2,64,64]{3,2,1,0:T(8,128)}, f32[4,64,64]{2,1,0:T(8,128)}) custom-call(f32[2,64,128]{2,1,0:T(8,128)} %copy-done.2, f32[2,64,128]{2,1,0:T(8,128)} %copy-done.3, f32[2,128,128]{2,1,0:T(8,128)} %get-tuple-element.9.refs_2_), custom_call_target="tpu_custom_call" | custom-call | tf_op jit(solution)/shard_map/factor/pallas_call | solution.py:189
  (2 shorter events, 0.0 us)
Async XLA Ops:
  28.5 7.1 %copy-start.1 = (f32[1024,64]{0,1:T(8,128)S(1)}, f32[1024,64]{0,1:T(8,128)}, u32[]{:S(2)}) copy-start(f32[1024,64]{0,1:T(8,128)} %param.4) | copy-start | bytes 786436
  28.5 36.4 %all-to-all-start = ((f32[128,32,128]{2,1,0:T(8,128)}), f32[128,32,128]{2,1,0:T(8,128)S(1)}, u32[]{:S(2)}, u32[]{:S(2)}) async-start(f32[128,32,128]{2,1,0:T(8,128)} %bitcast.6), calls=%async_computation | async-start | bytes 4194304 | tf_op jit(solution)/shard_map/all_to_all | solution.py:177
  64.9 1.3 %copy-start = (f32[128,32,128]{2,1,0:T(8,128)}, f32[128,32,128]{2,1,0:T(8,128)S(1)}, u32[]{:S(2)}) copy-start(f32[128,32,128]{2,1,0:T(8,128)S(1)} %all-to-all-done) | copy-start | bytes 6291460
  70.7 1.5 %collective-permute-start = (f32[2,64,128]{2,1,0:T(8,128)}, f32[2,64,128]{2,1,0:T(8,128)S(1)}, u32[]{:S(2)}, u32[]{:S(2)}) collective-permute-start(f32[2,64,128]{2,1,0:T(8,128)} %get-tuple-element.8), channel_id=1, source_target_pairs={{0,8},{8,0},{16,24},{24,16},{32,40},{40,32},{48,56},{56,48},{64,72... | collective-permute-start | bytes 196616 | tf_op jit(solution)/shard_map/ppermute | solution.py:186
  73.0 4.3 %collective-permute-start.1 = (f32[2,64,128]{2,1,0:T(8,128)S(1)}, f32[2,64,128]{2,1,0:T(8,128)S(1)}, u32[]{:S(2)}, u32[]{:S(2)}) collective-permute-start(f32[2,64,128]{2,1,0:T(8,128)S(1)} %add.9), channel_id=1, source_target_pairs={{0,64},{8,72},{16,80},{24,88},{32,96},{40,104},{48,112},{56,120},{... | collective-permute-start | bytes 196616 | tf_op jit(solution)/shard_map/ppermute | solution.py:186
  77.3 4.3 %collective-permute-start.2 = (f32[2,64,128]{2,1,0:T(8,128)S(1)}, f32[2,64,128]{2,1,0:T(8,128)S(1)}, u32[]{:S(2)}, u32[]{:S(2)}) collective-permute-start(f32[2,64,128]{2,1,0:T(8,128)S(1)} %add.10), channel_id=1, source_target_pairs={{0,16},{8,24},{16,0},{24,8},{32,48},{40,56},{48,32},{56,40},{64,80... | collective-permute-start | bytes 196616 | tf_op jit(solution)/shard_map/ppermute | solution.py:186
  81.7 5.6 %copy-start.2 = (f32[2,64,128]{2,1,0:T(8,128)}, f32[2,64,128]{2,1,0:T(8,128)S(1)}, u32[]{:S(2)}) copy-start(f32[2,64,128]{2,1,0:T(8,128)S(1)} %add.11.refs_0_) | copy-start | bytes 196612
  81.7 5.6 %collective-permute-start.3 = (f32[2,64,128]{2,1,0:T(8,128)S(1)}, f32[2,64,128]{2,1,0:T(8,128)S(1)}, u32[]{:S(2)}, u32[]{:S(2)}) collective-permute-start(f32[2,64,128]{2,1,0:T(8,128)S(1)} %add.11.refs_0_), channel_id=1, source_target_pairs={{0,48},{8,56},{16,32},{24,40},{32,16},{40,24},{48,0},{56,8},{64,11... | collective-permute-start | bytes 196616 | tf_op jit(solution)/shard_map/ppermute | solution.py:187
  87.3 0.6 copy-start.3

commit v2 on v1

v2 whole, which is shorter than its diff:
```python
import math

import jax
import jax.numpy as jnp
import numpy as np
from jax import lax
from jax.experimental import pallas as pl
from jax.experimental.pallas import tpu as pltpu
from jax.sharding import PartitionSpec as P


FREQS = 32
RANK = 64
F32 = jnp.float32
BF16 = jnp.bfloat16
NT = (((1,), (1,)), ((), ()))
NN = (((1,), (0,)), ((), ()))


def dft_rows(samples):
    times = np.arange(samples)
    orders = np.arange(1, FREQS + 1)
    angles = (orders[:, None] * times[None, :] % samples) * (2.0 * math.pi / samples)
    weights = np.stack([np.cos(angles), -np.sin(angles)], axis=1)
    return (weights.reshape(2 * FREQS, samples) / math.sqrt(samples)).astype(np.float32)


def small(mib):
    return dict(compiler_params=pltpu.CompilerParams(vmem_limit_bytes=mib << 20))


def split(x):
    high = x.astype(BF16)
    return high, (x - high.astype(F32)).astype(BF16)


def mm(a, b, dims):
    return lax.dot_general(a, b, dims, preferred_element_type=F32)


def low_lanes(shape):
    return lax.broadcasted_iota(jnp.int32, shape, 1) < 64


def dft_kernel(x_hbm, w_hbm, spec_hbm, x_ref, w_ref, out_ref, x_sems, w_sem, out_sems):
    steps = x_ref.shape[1] // 128
    ahead = 3

    def fetch(step):
        span = pl.ds(pl.multiple_of(128 * step, 128), 128)
        return pltpu.make_async_copy(x_hbm.at[:, span, :], x_ref.at[:, span, :], x_sems.at[step])

    def put(step):
        span = pl.ds(pl.multiple_of(16 * step, 16), 16)
        return pltpu.make_async_copy(out_ref.at[span], spec_hbm.at[span], out_sems.at[step])

    w_copy = pltpu.make_async_copy(w_hbm, w_ref, w_sem)
    w_copy.start()
    for step in range(ahead):
        fetch(step).start()
    w_copy.wait()

    def body(step, carry):
        fetch(step).wait()

        @pl.when(step + ahead < steps)
        def _():
            fetch(step + ahead).start()

        weights = w_ref[...]
        for tile in range(2):
            rows = pl.ds(pl.multiple_of(128 * step + 64 * tile, 64), 64)
            dest = pl.ds(pl.multiple_of(16 * step + 8 * tile, 8), 8)
            for half in range(2):
                high, low = split(x_ref[4 * half : 4 * half + 4, rows, :].reshape(256, -1))
                both = mm(weights, high, NT)
                out = both[:64] + both[64:] + mm(weights[:64], low, NT)
                for c in range(2):
                    out_ref[dest, 2 * half + c] = out[:, 128 * c : 128 * c + 128].reshape(8, 8, 128)
        put(step).start()
        return carry

    lax.fori_loop(0, steps, body, 0)
    for step in range(steps):
        put(step).wait()


def own_kernel(spec_ref, st_ref, *refs):
    d_ref = refs[-1]
    low_half = low_lanes((64, 128))
    zero = jnp.zeros((64, 128), F32)
    total = None
    for g in range(spec_ref.shape[0] // 16):
        rows = jnp.concatenate(
            [
                jnp.concatenate(
                    [spec_ref[16 * g + 8 * t : 16 * g + 8 * t + 8, a].reshape(64, 128) for t in range(2)], axis=1
                )
                for a in range(4)
            ],
            axis=0,
        )
        st = st_ref[:, 128 * g : 128 * g + 128]
        rolled = pltpu.roll(st, 64, 1)
        even = jnp.concatenate([jnp.where(low_half, st, zero), jnp.where(low_half, rolled, zero)], axis=1)
        odd = jnp.concatenate([jnp.where(low_half, zero, rolled), jnp.where(low_half, zero, st)], axis=1)
        s_high, s_low = split(jnp.concatenate([even, odd], axis=0))
        high, low = split(rows)
        both = mm(high, jnp.concatenate([s_high, s_low], axis=0), NT)
        out = both[:, :128] + both[:, 128:] + mm(low, s_high, NT)
        total = out if total is None else total + out

    @pl.when(pl.program_id(0) == 0)
    def _():
        d_ref[...] = jnp.zeros_like(d_ref)

    for a in range(4):
        d_ref[:, a] += total[64 * a : 64 * a + 64].reshape(8, 8, 128)

    @pl.when(pl.program_id(0) == pl.num_programs(0) - 1)
    def _():
        me = lax.axis_index("rcv")
        for slot, ref in enumerate(refs[:-1]):
            ref[...] = d_ref[slot ^ me]


def place_kernel(*refs):
    out_ref = refs[-1]
    me = lax.axis_index("rcv")
    low_half = low_lanes((4, 128))
    for slot, ref in enumerate(refs[:-1]):
        row = pl.multiple_of(8 * (slot ^ me), 8)
        for q in range(2):
            for p in range(2):
                first, second = ref[:, 4 * q + p, :], ref[:, 4 * q + 2 + p, :]
                even = jnp.where(low_half, first, pltpu.roll(second, 64, 1))
                odd = jnp.where(low_half, pltpu.roll(first, 64, 1), second)
                for a in range(4):
                    out_ref[q, pl.ds(64 * p + row + 2 * a, 1), :] = even[a : a + 1]
                    out_ref[q, pl.ds(64 * p + row + 2 * a + 1, 1), :] = odd[a : a + 1]


def sketch_kernel(r_ref, d_ref, s_ref, gram_ref, z_ref, acc_ref):
    step = pl.program_id(0)
    depth = r_ref.shape[0] // 8
    s_even = s_ref[pl.ds(0, depth, stride=2), :]
    s_odd = s_ref[pl.ds(1, depth, stride=2), :]
    s_high, s_low = split(jnp.transpose(jnp.concatenate([s_even, s_odd], axis=1)))
    s_both = jnp.concatenate([s_high, s_low], axis=0)

    @pl.when(step == 0)
    def _():
        acc_ref[...] = jnp.zeros_like(acc_ref)

    for pair in range(4):
        block = jnp.concatenate([r_ref[pl.ds(2 * pair + p, depth, stride=8), :] for p in range(2)], axis=1)
        high, low = split(block)
        both = mm(s_both, high, NN)
        acc_ref[pair] += both[:128] + both[128:] + mm(s_high, low, NN)

    @pl.when(step == pl.num_programs(0) - 1)
    def _():
        low_half = low_lanes((64, 128))
        for q in range(2):
            halves = []
            for f in range(2):
                sums = acc_ref[2 * q + f]
                x, y = sums[:, :128], sums[:, 128:]
                halves.append(
                    jnp.where(
                        low_half,
                        x[:64] + pltpu.roll(x[64:], 64, 1),
                        pltpu.roll(y[:64], 64, 1) + y[64:],
                    )
                )
            reverse = jnp.transpose(jnp.concatenate(halves, axis=0))
            z = 0.5 * (d_ref[q] + reverse)
            z_ref[q] = z
            gram = lax.dot_general(
                z, z, (((0,), (0,)), ((), ())), precision=lax.Precision.HIGHEST, preferred_element_type=F32
            )
            gram_ref[q] = jnp.where(low_half, gram[:64], gram[64:])


def factor_kernel(scaling, g_ref, h_ref, z_ref, basis_ref, r_ref, u_ref, l_ref):
    lane = lax.broadcasted_iota(jnp.int32, (8, 128), 1)
    sub = lax.broadcasted_iota(jnp.int32, (8, 128), 0)
    base = lane - lane % 64
    inner = lane % 64
    g = [[g_ref[q, 8 * b : 8 * b + 8, :] + h_ref[q, 8 * b : 8 * b + 8, :] for b in range(8)] for q in range(2)]
    e = [[jnp.where(inner == sub + 8 * b, 1.0, 0.0).astype(F32) for b in range(8)] for _ in range(2)]
    for j in range(64):
        top, row = j // 8, j % 8
        index = base + j
        for q in range(2):
            cols = {b: jnp.take_along_axis(g[q][b], index, axis=1) for b in range(top, 8)}
            pivot = jnp.broadcast_to(cols[top][row : row + 1], (8, 128))
            grow = jnp.broadcast_to(g[q][top][row : row + 1], (8, 128))
            erow = jnp.broadcast_to(e[q][top][row : row + 1], (8, 128))
            scale = lax.rsqrt(pivot)
            scale = scale * (1.5 - 0.5 * pivot * scale * scale)
            u_ref[q, j : j + 1, :] = jnp.where(inner >= j, grow * scale, 0.0)[:1]
            l_ref[q, j : j + 1, :] = (erow * scale)[:1]
            inverse = 1.0 / pivot
            grow = grow * inverse
            erow = erow * inverse
            for b in range(top, 8):
                c = cols[b]
                if b == top:
                    c = jnp.where(sub > row, c, 0.0)
                g[q][b] = g[q][b] - c * grow
                e[q][b] = e[q][b] - c * erow
    low_half = low_lanes((64, 128))
    for q in range(2):
        u = u_ref[q] * (1.0 / scaling)
        r_ref[2 * q] = u[:, :64]
        r_ref[2 * q + 1] = pltpu.roll(u, 64, 1)[:, :64]
        inv = l_ref[q]
        inv = jnp.concatenate([jnp.where(low_half, inv, 0.0), jnp.where(low_half, 0.0, inv)], axis=0)
        out = lax.dot_general(z_ref[q], inv, NT, precision=lax.Precision.HIGHEST, preferred_element_type=F32) * scaling
        turned = pltpu.roll(out, 64, 1)
        for p in range(2):
            basis_ref[2 * q, p] = out[64 * p : 64 * p + 64, :64]
            basis_ref[2 * q + 1, p] = turned[64 * p : 64 * p + 64, :64]


def local(traces, sketch):
    shots, receivers, samples = traces.shape
    devices = lax.axis_size("src") * lax.axis_size("rcv")
    rcv_count = lax.axis_size("rcv")
    weights = dft_rows(samples)
    w_high = weights.astype(BF16)
    w_low = (weights - w_high.astype(np.float32)).astype(BF16)
    w_both = jnp.asarray(np.concatenate([w_high, w_low], axis=0))
    sd = jax.ShapeDtypeStruct
    spec = pl.pallas_call(
        dft_kernel,
        in_specs=[pl.BlockSpec(memory_space=pltpu.HBM)] * 2,
        out_specs=pl.BlockSpec(memory_space=pltpu.HBM),
        out_shape=sd((devices, 4, 8, 128), F32),
        scratch_shapes=[
            pltpu.VMEM((shots, receivers, samples), F32),
            pltpu.VMEM((128, samples), BF16),
            pltpu.VMEM((devices, 4, 8, 128), F32),
            pltpu.SemaphoreType.DMA((receivers // 128,)),
            pltpu.SemaphoreType.DMA,
            pltpu.SemaphoreType.DMA((receivers // 128,)),
        ],
        cost_estimate=pl.CostEstimate(flops=3 * 2 * 64 * 8192 * 512, bytes_accessed=19 << 20, transcendentals=0),
        name="dft",
    )(traces, w_both)
    received = lax.all_to_all(spec.reshape(devices, 32, 128), ("src", "rcv"), split_axis=0, concat_axis=0, tiled=True)
    own = pl.pallas_call(
        own_kernel,
        grid=(2,),
        in_specs=[
            pl.BlockSpec((devices // 2, 4, 8, 128), lambda g: (g, 0, 0, 0)),
            pl.BlockSpec((RANK, receivers // 2), lambda g: (0, g)),
        ],
        out_specs=[pl.BlockSpec((4, 8, 128), lambda g: (0, 0, 0))] * rcv_count,
        out_shape=[sd((4, 8, 128), F32)] * rcv_count,
        scratch_shapes=[pltpu.VMEM((rcv_count, 4, 8, 128), F32)],
        cost_estimate=pl.CostEstimate(flops=3 << 30, bytes_accessed=4 << 20, transcendentals=0),
        name="own",
        **small(8),
    )
    pieces = list(own(pltpu.with_memory_space_constraint(spec, pltpu.HBM), sketch.T))
    for slot in range(1, rcv_count):
        pairs = [(r, r ^ slot) for r in range(rcv_count)]
        pieces[slot] = lax.ppermute(pieces[slot], "rcv", pairs)
    direct = pl.pallas_call(place_kernel, out_shape=sd((2, 128, 128), F32), name="place", **small(8))(*pieces)
    gram, z = pl.pallas_call(
        sketch_kernel,
        grid=(2,),
        in_specs=[
            pl.BlockSpec((devices * 16, 128), lambda g: (g, 0)),
            pl.BlockSpec((2, 128, 128), lambda g: (0, 0, 0)),
            pl.BlockSpec((receivers // 2, RANK), lambda g: (g, 0)),
        ],
        out_specs=[pl.BlockSpec((2, 64, 128), lambda g: (0, 0, 0)), pl.BlockSpec((2, 128, 128), lambda g: (0, 0, 0))],
        out_shape=[sd((2, 64, 128), F32), sd((2, 128, 128), F32)],
        scratch_shapes=[pltpu.VMEM((4, 128, 256), F32)],
        name="sketch",
        **small(12),
    )(pltpu.with_memory_space_constraint(received.reshape(devices * 32, 128), pltpu.VMEM), direct, sketch)
    src = lax.axis_size("src")
    for bits in (1, 8, 2):
        gram = gram + lax.ppermute(gram, "src", [(s, s ^ bits) for s in range(src)])
    other = lax.ppermute(gram, "src", [(s, s ^ 6) for s in range(src)])
    scaling = math.sqrt(2.0 * receivers)
    basis, r_factor = pl.pallas_call(
        lambda *refs: factor_kernel(scaling, *refs),
        out_shape=[sd((4, 2, 64, 64), F32), sd((4, 64, 64), F32)],
        scratch_shapes=[pltpu.VMEM((2, 64, 128), F32), pltpu.VMEM((2, 64, 128), F32)],
        name="factor",
        **small(8),
    )(gram, other, z)
    return basis, r_factor


def solution(mesh):
    in_specs = (P(("src", "rcv"), None, None), P())
    out_specs = (P("rcv", None, "src", None), P("rcv", None, None))
    return jax.shard_map(local, mesh=mesh, in_specs=in_specs, out_specs=out_specs, check_vma=False)
```

time: 95.9 us -> 81.6 us (0.85)
  starting transfers between devices: 8.97 us -> 34.6 us
  waiting for transfers between devices: 42.1 us -> 25.5 us
  blocking collectives: 15.1 us -> 0 us
  Pallas kernels: 24.8 us -> 20.3 us
  local copies, waits for them, and re-layouts: 2.95 us -> 0.2 us
    all_to_all x1, waiting for transfers between devices: 28.3 us -> 0.01 us  [local(): lax.all_to_all(spec.reshape(devices, 32, 128), ('src', 'rcv'), split_axis...]
    ppermute x0 -> x7, starting transfers between devices: none -> 17.4 us  [local(): pieces[slot] = lax.ppermute(pieces[slot], 'rcv', pairs)]
    ppermute x0 -> x7, waiting for transfers between devices: none -> 15.8 us  [local(): pieces[slot] = lax.ppermute(pieces[slot], 'rcv', pairs)]
    all_to_all x1 -> x0, blocking collectives: 15.1 us -> none  [local(): lax.all_to_all(own.reshape(rcv_count, 32, 128), 'rcv', split_axis=0, conc...]
    all_to_all x1, starting transfers between devices: 7.04 us -> 11.2 us  [local(): lax.all_to_all(spec.reshape(devices, 32, 128), ('src', 'rcv'), split_axis...]
    pallas_call x2 -> x4, Pallas kernels: 17.3 us -> 13.8 us  [the longest x1 9.38 us: local(): pl.pallas_call(dft_kernel, in_specs=[pl.BlockSpec(memory_space=pltpu.HBM)...]
    unnamed x9 -> x3, local copies, waits for them, and re-layouts: 2.95 us -> 0.2 us
    ppermute x1, starting transfers between devices: 0.89 us -> 3.46 us  [local(): other = lax.ppermute(gram, 'src', [(s, s ^ 6) for s in range(src)])]
  transfers between devices with their start and end apart: 5 -> 12, of which waited for: 5 -> 7; matrix products, arithmetic and copies ran while one was open for 1% -> 0% of each run, Pallas kernels for 0% -> 3%
where the time goes in v2:
time: 81.6 us; the launch traced here: 81.4 us
  starting transfers between devices  34.6 us (42%)
  waiting for transfers between devices  25.5 us (31%)
  Pallas kernels  20.3 us (25%)
    ppermute x7, starting transfers between devices, local(): pieces[slot] = lax.ppermute(pieces[slot], 'rcv', pairs)  17.4 us
    ppermute x7, waiting for transfers between devices, local(): pieces[slot] = lax.ppermute(pieces[slot], 'rcv', pairs)  15.8 us
    all_to_all x1, starting transfers between devices, local(): lax.all_to_all(spec.reshape(devices, 32, 128), ('src', 'rcv'), split_axis...  11.2 us
    pallas_call x1, Pallas kernels, local(): pl.pallas_call(dft_kernel, in_specs=[pl.BlockSpec(memory_space=pltpu.HBM)...  9.38 us
    ppermute x3, waiting for transfers between devices, local(): gram = gram + lax.ppermute(gram, 'src', [(s, s ^ bits) for s in range(src)])  7.48 us
    pallas_call x1, Pallas kernels, local(): pl.pallas_call(lambda *refs: factor_kernel(scaling, *refs), out_shape=[sd...  6.52 us
    ppermute x1, starting transfers between devices, local(): other = lax.ppermute(gram, 'src', [(s, s ^ 6) for s in range(src)])  3.46 us
    ppermute x3, starting transfers between devices, local(): gram = gram + lax.ppermute(gram, 'src', [(s, s ^ bits) for s in range(src)])  2.54 us
  transfers between devices with their start and end apart: 12, of which 7 were waited for; matrix products, arithmetic and copies ran while one was open for 0% of the time, Pallas kernels for 3%

profile of v2, /device:TPU:0, one launch (start us, length us, event | category | flops | bytes accessed | tf_op | source)
XLA Modules:
  0.0 81.4 jit_solution(2262477896803588368)
XLA Ops:
  0.6 9.4 %dft.1.spec_ref = f32[128,4,8,128]{3,2,1,0:T(8,128)} custom-call(f32[8,1024,512]{2,1,0:T(8,128)} %x_hbm.1, bf16[128,512]{1,0:T(8,128)(2,1)} %constant.2.clone.w_hbm), custom_call_target="tpu_custom_call" | custom-call | flops 1610612736 | bytes 19922944 | tf_op jit(solution)/shard_map/dft/pallas_call | solution.py:236
  10.0 0.0 copy-start
  10.0 11.2 %all-to-all-start = ((f32[128,32,128]{2,1,0:T(8,128)}), f32[128,32,128]{2,1,0:T(8,128)S(1)}, u32[]{:S(2)}, u32[]{:S(2)}) async-start(f32[128,32,128]{2,1,0:T(8,128)} %bitcast.5), calls=%async_computation | async-start | bytes 4194304 | tf_op jit(solution)/shard_map/all_to_all | solution.py:252
  21.2 0.0 copy-done
  21.2 2.4 %own.1 = (f32[4,8,128]{2,1,0:T(8,128)S(1)}, f32[4,8,128]{2,1,0:T(8,128)S(1)}, f32[4,8,128]{2,1,0:T(8,128)S(1)}, f32[4,8,128]{2,1,0:T(8,128)S(1)}, f32[4,8,128]{2...) custom-call(f32[128,4,8,128]{3,2,1,0:T(8,128)} %dft.1.spec_ref, ...), custom_call_target="tpu_custom_call" | custom-call | flops 3221225472 | bytes 4194304 | tf_op jit(solution)/shard_map/own/pallas_call | solution.py:267
  23.6 2.6 %collective-permute-start = (f32[4,8,128]{2,1,0:T(8,128)S(1)}, f32[4,8,128]{2,1,0:T(8,128)S(1)}, u32[]{:S(2)}, u32[]{:S(2)}) collective-permute-start(f32[4,8,128]{2,1,0:T(8,128)S(1)} %get-tuple-element.13), channel_id=1, source_target_pairs={{0,1},{1,0},{2,3},{3,2},{4,5},{5,4},{6,7},{7,6},{8,9},{9,8},{10,11... | collective-permute-start | bytes 49160 | tf_op jit(solution)/shard_map/ppermute | solution.py:270
  26.2 1.5 %collective-permute-start.1 = (f32[4,8,128]{2,1,0:T(8,128)S(1)}, f32[4,8,128]{2,1,0:T(8,128)S(1)}, u32[]{:S(2)}, u32[]{:S(2)}) collective-permute-start(f32[4,8,128]{2,1,0:T(8,128)S(1)} %get-tuple-element.14), channel_id=1, source_target_pairs={{0,2},{1,3},{2,0},{3,1},{4,6},{5,7},{6,4},{7,5},{8,10},{9,11},{10,... | collective-permute-start | bytes 49160 | tf_op jit(solution)/shard_map/ppermute | solution.py:270
  27.7 1.1 %collective-permute-start.2 = (f32[4,8,128]{2,1,0:T(8,128)S(1)}, f32[4,8,128]{2,1,0:T(8,128)S(1)}, u32[]{:S(2)}, u32[]{:S(2)}) collective-permute-start(f32[4,8,128]{2,1,0:T(8,128)S(1)} %get-tuple-element.15), channel_id=1, source_target_pairs={{0,3},{1,2},{2,1},{3,0},{4,7},{5,6},{6,5},{7,4},{8,11},{9,10},{10,... | collective-permute-start | bytes 49160 | tf_op jit(solution)/shard_map/ppermute | solution.py:270
  28.7 2.5 %collective-permute-start.3 = (f32[4,8,128]{2,1,0:T(8,128)S(1)}, f32[4,8,128]{2,1,0:T(8,128)S(1)}, u32[]{:S(2)}, u32[]{:S(2)}) collective-permute-start(f32[4,8,128]{2,1,0:T(8,128)S(1)} %get-tuple-element.16), channel_id=1, source_target_pairs={{0,4},{1,5},{2,6},{3,7},{4,0},{5,1},{6,2},{7,3},{8,12},{9,13},{10,... | collective-permute-start | bytes 49160 | tf_op jit(solution)/shard_map/ppermute | solution.py:270
  31.2 3.0 %collective-permute-start.4 = (f32[4,8,128]{2,1,0:T(8,128)S(1)}, f32[4,8,128]{2,1,0:T(8,128)S(1)}, u32[]{:S(2)}, u32[]{:S(2)}) collective-permute-start(f32[4,8,128]{2,1,0:T(8,128)S(1)} %get-tuple-element.17), channel_id=1, source_target_pairs={{0,5},{1,4},{2,7},{3,6},{4,1},{5,0},{6,3},{7,2},{8,13},{9,12},{10,... | collective-permute-start | bytes 49160 | tf_op jit(solution)/shard_map/ppermute | solution.py:270
  34.2 9.2 %collective-permute-done.refs_1_ = f32[4,8,128]{2,1,0:T(8,128)S(1)} collective-permute-done((f32[4,8,128]{2,1,0:T(8,128)S(1)}, f32[4,8,128]{2,1,0:T(8,128)S(1)}, u32[]{:S(2)}, u32[]{:S(2)}) %collective-permute-start) | collective-permute-done | bytes 16416 | tf_op jit(solution)/shard_map/ppermute | solution.py:270
  43.4 6.3 %collective-permute-start.5 = (f32[4,8,128]{2,1,0:T(8,128)S(1)}, f32[4,8,128]{2,1,0:T(8,128)S(1)}, u32[]{:S(2)}, u32[]{:S(2)}) collective-permute-start(f32[4,8,128]{2,1,0:T(8,128)S(1)} %get-tuple-element.18), channel_id=1, source_target_pairs={{0,6},{1,7},{2,4},{3,5},{4,2},{5,3},{6,0},{7,1},{8,14},{9,15},{10,... | collective-permute-start | bytes 49160 | tf_op jit(solution)/shard_map/ppermute | solution.py:270
  49.7 0.0 collective-permute-done.1.refs_2_
  49.7 0.6 collective-permute-start.6
  50.3 0.2 copy.5.s_ref
  50.5 0.0 collective-permute-done.2.refs_3_
  50.5 0.0 collective-permute-done.3.refs_4_
  50.5 0.0 collective-permute-done.4.refs_5_
  50.6 0.9 %collective-permute-done.5.refs_6_ = f32[4,8,128]{2,1,0:T(8,128)S(1)} collective-permute-done((f32[4,8,128]{2,1,0:T(8,128)S(1)}, f32[4,8,128]{2,1,0:T(8,128)S(1)}, u32[]{:S(2)}, u32[]{:S(2)}) %collective-permute-start.5) | collective-permute-done | bytes 16416 | tf_op jit(solution)/shard_map/ppermute | solution.py:270
  51.4 5.6 %collective-permute-done.6.refs_7_ = f32[4,8,128]{2,1,0:T(8,128)S(1)} collective-permute-done((f32[4,8,128]{2,1,0:T(8,128)S(1)}, f32[4,8,128]{2,1,0:T(8,128)S(1)}, u32[]{:S(2)}, u32[]{:S(2)}) %collective-permute-start.6) | collective-permute-done | bytes 16416 | tf_op jit(solution)/shard_map/ppermute | solution.py:270
  57.1 0.1 place.1.d_ref
  57.2 0.0 all-to-all-done
  57.2 1.9 %sketch.1 = (f32[2,64,128]{2,1,0:T(8,128)S(1)}, f32[2,128,128]{2,1,0:T(8,128)S(1)}) custom-call(f32[4096,128]{1,0:T(8,128)S(1)} %bitcast.3, f32[2,128,128]{2,1,0:T(8,128)S(1)} %place.1.d_ref, f32[1024,64]{1,0:T(8,128)S(1)} %copy.5.s_ref), custom_call_target="tpu_custom_call" | custom-call | tf_op jit(solution)/shard_map/sketch/pallas_call | solution.py:272
  59.1 0.1 collective-permute-start.7
  59.2 1.2 %collective-permute-done.7 = f32[2,64,128]{2,1,0:T(8,128)S(1)} collective-permute-done((f32[2,64,128]{2,1,0:T(8,128)S(1)}, f32[2,64,128]{2,1,0:T(8,128)S(1)}, u32[]{:S(2)}, u32[]{:S(2)}) %collective-permute-start.7) | collective-permute-done | bytes 65568 | tf_op jit(solution)/shard_map/ppermute | solution.py:288
  60.5 0.7 collective-permute-start.8
  61.1 3.7 %collective-permute-done.8 = f32[2,64,128]{2,1,0:T(8,128)S(1)} collective-permute-done((f32[2,64,128]{2,1,0:T(8,128)S(1)}, f32[2,64,128]{2,1,0:T(8,128)S(1)}, u32[]{:S(2)}, u32[]{:S(2)}) %collective-permute-start.8) | collective-permute-done | bytes 65568 | tf_op jit(solution)/shard_map/ppermute | solution.py:288
  64.8 1.8 %collective-permute-start.9 = (f32[2,64,128]{2,1,0:T(8,128)S(1)}, f32[2,64,128]{2,1,0:T(8,128)S(1)}, u32[]{:S(2)}, u32[]{:S(2)}) collective-permute-start(f32[2,64,128]{2,1,0:T(8,128)S(1)} %add.10), channel_id=1, source_target_pairs={{0,16},{8,24},{16,0},{24,8},{32,48},{40,56},{48,32},{56,40},{64,80... | collective-permute-start | bytes 196616 | tf_op jit(solution)/shard_map/ppermute | solution.py:288
  66.6 2.6 %collective-permute-done.9 = f32[2,64,128]{2,1,0:T(8,128)S(1)} collective-permute-done((f32[2,64,128]{2,1,0:T(8,128)S(1)}, f32[2,64,128]{2,1,0:T(8,128)S(1)}, u32[]{:S(2)}, u32[]{:S(2)}) %collective-permute-start.9) | collective-permute-done | bytes 65568 | tf_op jit(solution)/shard_map/ppermute | solution.py:288
  69.2 3.5 %collective-permute-start.10 = (f32[2,64,128]{2,1,0:T(8,128)S(1)}, f32[2,64,128]{2,1,0:T(8,128)S(1)}, u32[]{:S(2)}, u32[]{:S(2)}) collective-permute-start(f32[2,64,128]{2,1,0:T(8,128)S(1)} %add.11.refs_0_), channel_id=1, source_target_pairs={{0,48},{8,56},{16,32},{24,40},{32,16},{40,24},{48,0},{56,8},{64,11... | collective-permute-start | bytes 196616 | tf_op jit(solution)/shard_map/ppermute | solution.py:289
  72.6 2.2 %collective-permute-done.10.refs_1_ = f32[2,64,128]{2,1,0:T(8,128)S(1)} collective-permute-done((f32[2,64,128]{2,1,0:T(8,128)S(1)}, f32[2,64,128]{2,1,0:T(8,128)S(1)}, u32[]{:S(2)}, u32[]{:S(2)}) %collective-permute-start.10) | collective-permute-done | bytes 65568 | tf_op jit(solution)/shard_map/ppermute | solution.py:289
  74.9 6.5 %factor.1 = (f32[4,2,64,64]{3,2,1,0:T(8,128)}, f32[4,64,64]{2,1,0:T(8,128)}) custom-call(f32[2,64,128]{2,1,0:T(8,128)S(1)} %add.11.refs_0_, f32[2,64,128]{2,1,0:T(8,128)S(1)} %collective-permute-done.10.refs_1_, f32[2,128,128]{2,1,0:T(8,128)S(1)} %get-tuple-element.21.refs_2_), custom_call_target="tpu_custom_call" | custom-call | tf_op jit(solution)/shard_map/factor/pallas_call | solution.py:291
  (3 shorter events, 0.0 us)
Async XLA Ops:
  10.0 11.2 %copy-start = (f32[1024,64]{0,1:T(8,128)S(1)}, f32[1024,64]{0,1:T(8,128)}, u32[]{:S(2)}) copy-start(f32[1024,64]{0,1:T(8,128)} %param.4) | copy-start | bytes 786436
  10.0 47.2 %all-to-all-start = ((f32[128,32,128]{2,1,0:T(8,128)}), f32[128,32,128]{2,1,0:T(8,128)S(1)}, u32[]{:S(2)}, u32[]{:S(2)}) async-start(f32[128,32,128]{2,1,0:T(8,128)} %bitcast.5), calls=%async_computation | async-start | bytes 4194304 | tf_op jit(solution)/shard_map/all_to_all | solution.py:252
  23.6 19.8 %collective-permute-start = (f32[4,8,128]{2,1,0:T(8,128)S(1)}, f32[4,8,128]{2,1,0:T(8,128)S(1)}, u32[]{:S(2)}, u32[]{:S(2)}) collective-permute-start(f32[4,8,128]{2,1,0:T(8,128)S(1)} %get-tuple-element.13), channel_id=1, source_target_pairs={{0,1},{1,0},{2,3},{3,2},{4,5},{5,4},{6,7},{7,6},{8,9},{9,8},{10,11... | collective-permute-start | bytes 49160 | tf_op jit(solution)/shard_map/ppermute | solution.py:270
  26.2 23.5 %collective-permute-start.1 = (f32[4,8,128]{2,1,0:T(8,128)S(1)}, f32[4,8,128]{2,1,0:T(8,128)S(1)}, u32[]{:S(2)}, u32[]{:S(2)}) collective-permute-start(f32[4,8,128]{2,1,0:T(8,128)S(1)} %get-tuple-element.14), channel_id=1, source_target_pairs={{0,2},{1,3},{2,0},{3,1},{4,6},{5,7},{6,4},{7,5},{8,10},{9,11},{10,... | collective-permute-start | bytes 49160 | tf_op jit(solution)/shard_map/ppermute | solution.py:270
  27.7 22.9 %collective-permute-start.2 = (f32[4,8,128]{2,1,0:T(8,128)S(1)}, f32[4,8,128]{2,1,0:T(8,128)S(1)}, u32[]{:S(2)}, u32[]{:S(2)}) collective-permute-start(f32[4,8,128]{2,1,0:T(8,128)S(1)} %get-tuple-element.15), channel_id=1, source_target_pairs={{0,3},{1,2},{2,1},{3,0},{4,7},{5,6},{6,5},{7,4},{8,11},{9,10},{10,... | collective-permute-start | bytes 49160 | tf_op jit(solution)/shard_map/ppermute | solution.py:270
  28.7 21.8 %collective-permute-start.3 = (f32[4,8,128]{2,1,0:T(8,128)S(1)}, f32[4,8,128]{2,1,0:T(8,128)S(1)}, u32[]{:S(2)}, u32[]{:S(2)}) collective-permute-start(f32[4,8,128]{2,1,0:T(8,128)S(1)} %get-tuple-element.16), channel_id=1, source_target_pairs={{0,4},{1,5},{2,6},{3,7},{4,0},{5,1},{6,2},{7,3},{8,12},{9,13},{10,... | collective-permute-start | bytes 49160 | tf_op jit(solution)/shard_map/ppermute | solution.py:270
  31.2 19.4 %collective-permute-start.4 = (f32[4,8,128]{2,1,0:T(8,128)S(1)}, f32[4,8,128]{2,1,0:T(8,128)S(1)}, u32[]{:S(2)}, u32[]{:S(2)}) collective-permute-start(f32[4,8,128]{2,1,0:T(8,128)S(1)} %get-tuple-element.17), channel_id=1, source_target_pairs={{0,5},{1,4},{2,7},{3,6},{4,1},{5,0},{6,3},{7,2},{8,13},{9,12},{10,... | collective-permute-start | bytes 49160 | tf_op jit(solution)/shard_map/ppermute | solution.py:270
  43.4 8.0 %collective-permute-start.5 = (f32[4,8,128]{2,1,0:T(8,128)S(1)}, f32[4,8,128]{2,1,0:T(8,128)S(1)}, u32[]{:S(2)}, u32[]{:S(2)}) collective-permute-start(f32[4,8,128]{2,1,0:T(8,128)S(1)} %get-tuple-element.18), channel_id=1, source_target_pairs={{0,6},{1,7},{2,4},{3,5},{4,2},{5,3},{6,0},{7,1},{8,14},{9,15},{10,... | collective-permute-start | bytes 49160 | tf_op jit(solution)/shard_map/ppermute | solution.py:270
  49.7 7.4 %collective-permute-start.6 = (f32[4,8,128]{2,1,0:T(8,128)S(1)}, f32[4,8,128]{2,1,0:T(8,128)S(1)}, u32[]{:S(2)}, u32[]{:S(2)}) collective-permute-start(f32[4,8,128]{2,1,0:T(8,128)S(1)} %get-tuple-element.19), channel_id=1, source_target_pairs={{0,7},{1,6},{2,5},{3,4},{4,3},{5,2},{6,1},{7,0},{8,15},{9,14},{10,... | collective-permute-start | bytes 49160 | tf_op jit(solution)/shard_map/ppermute | solution.py:270
  59.1 1.3 %collective-permute-start.7 = (f32[2,64,128]{2,1,0:T(8,128)S(1)}, f32[2,64,128]{2,1,0:T(8,128)S(1)}, u32[]{:S(2)}, u32[]{:S(2)}) collective-permute-start(f32[2,64,128]{2,1,0:T(8,128)S(1)} %get-tuple-element.20), channel_id=1, source_target_pairs={{0,8},{8,0},{16,24},{24,16},{32,40},{40,32},{48,56},{56,48},{64,72... | collective-permute-start | bytes 196616 | tf_op jit(solution)/shard_map/ppermute | solution.py:288
  60.5 4.3 %collective-permute-start.8 = (f32[2,64,128]{2,1,0:T(8,128)S(1)}, f32[2,64,128]{2,1,0:T(8,128)S(1)}, u32[]{:S(2)}, u32[]{:S(2)}) collective-permute-start(f32[2,64,128]{2,1,0:T(8,128)S(1)} %add.9), channel_id=1, source_target_pairs={{0,64},{8,72},{16,80},{24,88},{32,96},{40,104},{48,112},{56,120},{... | collective-permute-start | bytes 196616 | tf_op jit(solution)/shard_map/ppermute | solution.py:288
  64.8 4.3 %collective-permute-start.9 = (f32[2,64,128]{2,1,0:T(8,128)S(1)}, f32[2,64,128]{2,1,0:T(8,128)S(1)}, u32[]{:S(2)}, u32[]{:S(2)}) collective-permute-start(f32[2,64,128]{2,1,0:T(8,128)S(1)} %add.10), channel_id=1, source_target_pairs={{0,16},{8,24},{16,0},{24,8},{32,48},{40,56},{48,32},{56,40},{64,80... | collective-permute-start | bytes 196616 | tf_op jit(solution)/shard_map/ppermute | solution.py:288
  69.2 5.7 %collective-permute-start.10 = (f32[2,64,128]{2,1,0:T(8,128)S(1)}, f32[2,64,128]{2,1,0:T(8,128)S(1)}, u32[]{:S(2)}, u32[]{:S(2)}) collective-permute-start(f32[2,64,128]{2,1,0:T(8,128)S(1)} %add.11.refs_0_), channel_id=1, source_target_pairs={{0,48},{8,56},{16,32},{24,40},{32,16},{40,24},{48,0},{56,8},{64,11... | collective-permute-start | bytes 196616 | tf_op jit(solution)/shard_map/ppermute | solution.py:289

commit v3 on v2

--- a/solution.py
+++ b/solution.py
@@ -189,27 +189,34 @@
     inner = lane % 64
     g = [[g_ref[q, 8 * b : 8 * b + 8, :] + h_ref[q, 8 * b : 8 * b + 8, :] for b in range(8)] for q in range(2)]
     e = [[jnp.where(inner == sub + 8 * b, 1.0, 0.0).astype(F32) for b in range(8)] for _ in range(2)]
-    for j in range(64):
-        top, row = j // 8, j % 8
-        index = base + j
-        for q in range(2):
-            cols = {b: jnp.take_along_axis(g[q][b], index, axis=1) for b in range(top, 8)}
-            pivot = jnp.broadcast_to(cols[top][row : row + 1], (8, 128))
-            grow = jnp.broadcast_to(g[q][top][row : row + 1], (8, 128))
-            erow = jnp.broadcast_to(e[q][top][row : row + 1], (8, 128))
-            scale = lax.rsqrt(pivot)
-            scale = scale * (1.5 - 0.5 * pivot * scale * scale)
-            u_ref[q, j : j + 1, :] = jnp.where(inner >= j, grow * scale, 0.0)[:1]
-            l_ref[q, j : j + 1, :] = (erow * scale)[:1]
-            inverse = 1.0 / pivot
-            grow = grow * inverse
-            erow = erow * inverse
-            for b in range(top, 8):
-                c = cols[b]
-                if b == top:
-                    c = jnp.where(sub > row, c, 0.0)
-                g[q][b] = g[q][b] - c * grow
-                e[q][b] = e[q][b] - c * erow
+
+    def spread(x, row):
+        return jnp.broadcast_to(x[row : row + 1], (8, 128))
+
+    for top in range(8):
+        cols = [
+            [[jnp.take_along_axis(g[q][b], base + (8 * top + a), axis=1) for b in range(top, 8)] for a in range(8)]
+            for q in range(2)
+        ]
+        for a in range(8):
+            j = 8 * top + a
+            for q in range(2):
+                pivot = spread(cols[q][a][0], a)
+                inverse = 1.0 / pivot
+                mult = [x * inverse for x in cols[q][a]]
+                for later in range(a + 1, 8):
+                    weight = spread(cols[q][later][0], a)
+                    cols[q][later] = [x - m * weight for x, m in zip(cols[q][later], mult)]
+                grow = spread(g[q][top], a)
+                erow = spread(e[q][top], a)
+                scale = lax.rsqrt(pivot)
+                scale = scale * (1.5 - 0.5 * pivot * scale * scale)
+                u_ref[q, j : j + 1, :] = jnp.where(inner >= j, grow * scale, 0.0)[:1]
+                l_ref[q, j : j + 1, :] = (erow * scale)[:1]
+                mult[0] = jnp.where(sub > a, mult[0], 0.0)
+                for b in range(top, 8):
+                    g[q][b] = g[q][b] - mult[b - top] * grow
+                    e[q][b] = e[q][b] - mult[b - top] * erow
     low_half = low_lanes((64, 128))
     for q in range(2):
         u = u_ref[q] * (1.0 / scaling)

time: 81.6 us -> 78.3 us (0.960)
  Pallas kernels: 20.3 us -> 17 us
    pallas_call x1, Pallas kernels: 6.52 us -> 3.24 us  [local(): pl.pallas_call(lambda *refs: factor_kernel(scaling, *refs), out_shape=[sd...]
where the time goes in v3:
time: 78.3 us; the launch traced here: 78.1 us
  starting transfers between devices  34.6 us (44%)
  waiting for transfers between devices  25.5 us (33%)
  Pallas kernels  17 us (22%)
    ppermute x7, starting transfers between devices, local(): pieces[slot] = lax.ppermute(pieces[slot], 'rcv', pairs)  17.4 us
    ppermute x7, waiting for transfers between devices, local(): pieces[slot] = lax.ppermute(pieces[slot], 'rcv', pairs)  15.8 us
    all_to_all x1, starting transfers between devices, local(): lax.all_to_all(spec.reshape(devices, 32, 128), ('src', 'rcv'), split_axis...  11.2 us
    pallas_call x1, Pallas kernels, local(): pl.pallas_call(dft_kernel, in_specs=[pl.BlockSpec(memory_space=pltpu.HBM)...  9.38 us
    ppermute x3, waiting for transfers between devices, local(): gram = gram + lax.ppermute(gram, 'src', [(s, s ^ bits) for s in range(src)])  7.48 us
    ppermute x1, starting transfers between devices, local(): other = lax.ppermute(gram, 'src', [(s, s ^ 6) for s in range(src)])  3.46 us
    pallas_call x1, Pallas kernels, local(): pl.pallas_call(lambda *refs: factor_kernel(scaling, *refs), out_shape=[sd...  3.24 us
    ppermute x3, starting transfers between devices, local(): gram = gram + lax.ppermute(gram, 'src', [(s, s ^ bits) for s in range(src)])  2.54 us
  transfers between devices with their start and end apart: 12, of which 7 were waited for; matrix products, arithmetic and copies ran while one was open for 0% of the time, Pallas kernels for 3%

profile of v3, /device:TPU:0, one launch (start us, length us, event | category | flops | bytes accessed | tf_op | source)
XLA Modules:
  0.0 78.1 jit_solution(10170404760328583835)
XLA Ops:
  0.6 9.4 %dft.1.spec_ref = f32[128,4,8,128]{3,2,1,0:T(8,128)} custom-call(f32[8,1024,512]{2,1,0:T(8,128)} %x_hbm.1, bf16[128,512]{1,0:T(8,128)(2,1)} %constant.2.clone.w_hbm), custom_call_target="tpu_custom_call" | custom-call | flops 1610612736 | bytes 19922944 | tf_op jit(solution)/shard_map/dft/pallas_call | solution.py:243
  10.0 0.0 copy-start
  10.0 11.2 %all-to-all-start = ((f32[128,32,128]{2,1,0:T(8,128)}), f32[128,32,128]{2,1,0:T(8,128)S(1)}, u32[]{:S(2)}, u32[]{:S(2)}) async-start(f32[128,32,128]{2,1,0:T(8,128)} %bitcast.5), calls=%async_computation | async-start | bytes 4194304 | tf_op jit(solution)/shard_map/all_to_all | solution.py:259
  21.2 0.0 copy-done
  21.2 2.4 %own.1 = (f32[4,8,128]{2,1,0:T(8,128)S(1)}, f32[4,8,128]{2,1,0:T(8,128)S(1)}, f32[4,8,128]{2,1,0:T(8,128)S(1)}, f32[4,8,128]{2,1,0:T(8,128)S(1)}, f32[4,8,128]{2...) custom-call(f32[128,4,8,128]{3,2,1,0:T(8,128)} %dft.1.spec_ref, ...), custom_call_target="tpu_custom_call" | custom-call | flops 3221225472 | bytes 4194304 | tf_op jit(solution)/shard_map/own/pallas_call | solution.py:274
  23.6 2.6 %collective-permute-start = (f32[4,8,128]{2,1,0:T(8,128)S(1)}, f32[4,8,128]{2,1,0:T(8,128)S(1)}, u32[]{:S(2)}, u32[]{:S(2)}) collective-permute-start(f32[4,8,128]{2,1,0:T(8,128)S(1)} %get-tuple-element.13), channel_id=1, source_target_pairs={{0,1},{1,0},{2,3},{3,2},{4,5},{5,4},{6,7},{7,6},{8,9},{9,8},{10,11... | collective-permute-start | bytes 49160 | tf_op jit(solution)/shard_map/ppermute | solution.py:277
  26.2 1.5 %collective-permute-start.1 = (f32[4,8,128]{2,1,0:T(8,128)S(1)}, f32[4,8,128]{2,1,0:T(8,128)S(1)}, u32[]{:S(2)}, u32[]{:S(2)}) collective-permute-start(f32[4,8,128]{2,1,0:T(8,128)S(1)} %get-tuple-element.14), channel_id=1, source_target_pairs={{0,2},{1,3},{2,0},{3,1},{4,6},{5,7},{6,4},{7,5},{8,10},{9,11},{10,... | collective-permute-start | bytes 49160 | tf_op jit(solution)/shard_map/ppermute | solution.py:277
  27.7 1.1 %collective-permute-start.2 = (f32[4,8,128]{2,1,0:T(8,128)S(1)}, f32[4,8,128]{2,1,0:T(8,128)S(1)}, u32[]{:S(2)}, u32[]{:S(2)}) collective-permute-start(f32[4,8,128]{2,1,0:T(8,128)S(1)} %get-tuple-element.15), channel_id=1, source_target_pairs={{0,3},{1,2},{2,1},{3,0},{4,7},{5,6},{6,5},{7,4},{8,11},{9,10},{10,... | collective-permute-start | bytes 49160 | tf_op jit(solution)/shard_map/ppermute | solution.py:277
  28.7 2.5 %collective-permute-start.3 = (f32[4,8,128]{2,1,0:T(8,128)S(1)}, f32[4,8,128]{2,1,0:T(8,128)S(1)}, u32[]{:S(2)}, u32[]{:S(2)}) collective-permute-start(f32[4,8,128]{2,1,0:T(8,128)S(1)} %get-tuple-element.16), channel_id=1, source_target_pairs={{0,4},{1,5},{2,6},{3,7},{4,0},{5,1},{6,2},{7,3},{8,12},{9,13},{10,... | collective-permute-start | bytes 49160 | tf_op jit(solution)/shard_map/ppermute | solution.py:277
  31.2 3.0 %collective-permute-start.4 = (f32[4,8,128]{2,1,0:T(8,128)S(1)}, f32[4,8,128]{2,1,0:T(8,128)S(1)}, u32[]{:S(2)}, u32[]{:S(2)}) collective-permute-start(f32[4,8,128]{2,1,0:T(8,128)S(1)} %get-tuple-element.17), channel_id=1, source_target_pairs={{0,5},{1,4},{2,7},{3,6},{4,1},{5,0},{6,3},{7,2},{8,13},{9,12},{10,... | collective-permute-start | bytes 49160 | tf_op jit(solution)/shard_map/ppermute | solution.py:277
  34.2 9.2 %collective-permute-done.refs_1_ = f32[4,8,128]{2,1,0:T(8,128)S(1)} collective-permute-done((f32[4,8,128]{2,1,0:T(8,128)S(1)}, f32[4,8,128]{2,1,0:T(8,128)S(1)}, u32[]{:S(2)}, u32[]{:S(2)}) %collective-permute-start) | collective-permute-done | bytes 16416 | tf_op jit(solution)/shard_map/ppermute | solution.py:277
  43.4 6.3 %collective-permute-start.5 = (f32[4,8,128]{2,1,0:T(8,128)S(1)}, f32[4,8,128]{2,1,0:T(8,128)S(1)}, u32[]{:S(2)}, u32[]{:S(2)}) collective-permute-start(f32[4,8,128]{2,1,0:T(8,128)S(1)} %get-tuple-element.18), channel_id=1, source_target_pairs={{0,6},{1,7},{2,4},{3,5},{4,2},{5,3},{6,0},{7,1},{8,14},{9,15},{10,... | collective-permute-start | bytes 49160 | tf_op jit(solution)/shard_map/ppermute | solution.py:277
  49.7 0.0 collective-permute-done.1.refs_2_
  49.7 0.6 collective-permute-start.6
  50.3 0.2 copy.5.s_ref
  50.5 0.0 collective-permute-done.2.refs_3_
  50.5 0.0 collective-permute-done.3.refs_4_
  50.5 0.0 collective-permute-done.4.refs_5_
  50.6 0.9 %collective-permute-done.5.refs_6_ = f32[4,8,128]{2,1,0:T(8,128)S(1)} collective-permute-done((f32[4,8,128]{2,1,0:T(8,128)S(1)}, f32[4,8,128]{2,1,0:T(8,128)S(1)}, u32[]{:S(2)}, u32[]{:S(2)}) %collective-permute-start.5) | collective-permute-done | bytes 16416 | tf_op jit(solution)/shard_map/ppermute | solution.py:277
  51.4 5.6 %collective-permute-done.6.refs_7_ = f32[4,8,128]{2,1,0:T(8,128)S(1)} collective-permute-done((f32[4,8,128]{2,1,0:T(8,128)S(1)}, f32[4,8,128]{2,1,0:T(8,128)S(1)}, u32[]{:S(2)}, u32[]{:S(2)}) %collective-permute-start.6) | collective-permute-done | bytes 16416 | tf_op jit(solution)/shard_map/ppermute | solution.py:277
  57.1 0.1 place.1.d_ref
  57.2 0.0 all-to-all-done
  57.2 1.9 %sketch.1 = (f32[2,64,128]{2,1,0:T(8,128)S(1)}, f32[2,128,128]{2,1,0:T(8,128)S(1)}) custom-call(f32[4096,128]{1,0:T(8,128)S(1)} %bitcast.3, f32[2,128,128]{2,1,0:T(8,128)S(1)} %place.1.d_ref, f32[1024,64]{1,0:T(8,128)S(1)} %copy.5.s_ref), custom_call_target="tpu_custom_call" | custom-call | tf_op jit(solution)/shard_map/sketch/pallas_call | solution.py:279
  59.1 0.1 collective-permute-start.7
  59.2 1.2 %collective-permute-done.7 = f32[2,64,128]{2,1,0:T(8,128)S(1)} collective-permute-done((f32[2,64,128]{2,1,0:T(8,128)S(1)}, f32[2,64,128]{2,1,0:T(8,128)S(1)}, u32[]{:S(2)}, u32[]{:S(2)}) %collective-permute-start.7) | collective-permute-done | bytes 65568 | tf_op jit(solution)/shard_map/ppermute | solution.py:295
  60.5 0.7 collective-permute-start.8
  61.1 3.7 %collective-permute-done.8 = f32[2,64,128]{2,1,0:T(8,128)S(1)} collective-permute-done((f32[2,64,128]{2,1,0:T(8,128)S(1)}, f32[2,64,128]{2,1,0:T(8,128)S(1)}, u32[]{:S(2)}, u32[]{:S(2)}) %collective-permute-start.8) | collective-permute-done | bytes 65568 | tf_op jit(solution)/shard_map/ppermute | solution.py:295
  64.8 1.8 %collective-permute-start.9 = (f32[2,64,128]{2,1,0:T(8,128)S(1)}, f32[2,64,128]{2,1,0:T(8,128)S(1)}, u32[]{:S(2)}, u32[]{:S(2)}) collective-permute-start(f32[2,64,128]{2,1,0:T(8,128)S(1)} %add.10), channel_id=1, source_target_pairs={{0,16},{8,24},{16,0},{24,8},{32,48},{40,56},{48,32},{56,40},{64,80... | collective-permute-start | bytes 196616 | tf_op jit(solution)/shard_map/ppermute | solution.py:295
  66.6 2.6 %collective-permute-done.9 = f32[2,64,128]{2,1,0:T(8,128)S(1)} collective-permute-done((f32[2,64,128]{2,1,0:T(8,128)S(1)}, f32[2,64,128]{2,1,0:T(8,128)S(1)}, u32[]{:S(2)}, u32[]{:S(2)}) %collective-permute-start.9) | collective-permute-done | bytes 65568 | tf_op jit(solution)/shard_map/ppermute | solution.py:295
  69.2 3.5 %collective-permute-start.10 = (f32[2,64,128]{2,1,0:T(8,128)S(1)}, f32[2,64,128]{2,1,0:T(8,128)S(1)}, u32[]{:S(2)}, u32[]{:S(2)}) collective-permute-start(f32[2,64,128]{2,1,0:T(8,128)S(1)} %add.11.refs_0_), channel_id=1, source_target_pairs={{0,48},{8,56},{16,32},{24,40},{32,16},{40,24},{48,0},{56,8},{64,11... | collective-permute-start | bytes 196616 | tf_op jit(solution)/shard_map/ppermute | solution.py:296
  72.6 2.2 %collective-permute-done.10.refs_1_ = f32[2,64,128]{2,1,0:T(8,128)S(1)} collective-permute-done((f32[2,64,128]{2,1,0:T(8,128)S(1)}, f32[2,64,128]{2,1,0:T(8,128)S(1)}, u32[]{:S(2)}, u32[]{:S(2)}) %collective-permute-start.10) | collective-permute-done | bytes 65568 | tf_op jit(solution)/shard_map/ppermute | solution.py:296
  74.9 3.2 %factor.1 = (f32[4,2,64,64]{3,2,1,0:T(8,128)}, f32[4,64,64]{2,1,0:T(8,128)}) custom-call(f32[2,64,128]{2,1,0:T(8,128)S(1)} %add.11.refs_0_, f32[2,64,128]{2,1,0:T(8,128)S(1)} %collective-permute-done.10.refs_1_, f32[2,128,128]{2,1,0:T(8,128)S(1)} %get-tuple-element.21.refs_2_), custom_call_target="tpu_custom_call" | custom-call | tf_op jit(solution)/shard_map/factor/pallas_call | solution.py:298
  (3 shorter events, 0.0 us)
Async XLA Ops:
  10.0 11.2 %copy-start = (f32[1024,64]{0,1:T(8,128)S(1)}, f32[1024,64]{0,1:T(8,128)}, u32[]{:S(2)}) copy-start(f32[1024,64]{0,1:T(8,128)} %param.4) | copy-start | bytes 786436
  10.0 47.2 %all-to-all-start = ((f32[128,32,128]{2,1,0:T(8,128)}), f32[128,32,128]{2,1,0:T(8,128)S(1)}, u32[]{:S(2)}, u32[]{:S(2)}) async-start(f32[128,32,128]{2,1,0:T(8,128)} %bitcast.5), calls=%async_computation | async-start | bytes 4194304 | tf_op jit(solution)/shard_map/all_to_all | solution.py:259
  23.6 19.8 %collective-permute-start = (f32[4,8,128]{2,1,0:T(8,128)S(1)}, f32[4,8,128]{2,1,0:T(8,128)S(1)}, u32[]{:S(2)}, u32[]{:S(2)}) collective-permute-start(f32[4,8,128]{2,1,0:T(8,128)S(1)} %get-tuple-element.13), channel_id=1, source_target_pairs={{0,1},{1,0},{2,3},{3,2},{4,5},{5,4},{6,7},{7,6},{8,9},{9,8},{10,11... | collective-permute-start | bytes 49160 | tf_op jit(solution)/shard_map/ppermute | solution.py:277
  26.2 23.5 %collective-permute-start.1 = (f32[4,8,128]{2,1,0:T(8,128)S(1)}, f32[4,8,128]{2,1,0:T(8,128)S(1)}, u32[]{:S(2)}, u32[]{:S(2)}) collective-permute-start(f32[4,8,128]{2,1,0:T(8,128)S(1)} %get-tuple-element.14), channel_id=1, source_target_pairs={{0,2},{1,3},{2,0},{3,1},{4,6},{5,7},{6,4},{7,5},{8,10},{9,11},{10,... | collective-permute-start | bytes 49160 | tf_op jit(solution)/shard_map/ppermute | solution.py:277
  27.7 22.9 %collective-permute-start.2 = (f32[4,8,128]{2,1,0:T(8,128)S(1)}, f32[4,8,128]{2,1,0:T(8,128)S(1)}, u32[]{:S(2)}, u32[]{:S(2)}) collective-permute-start(f32[4,8,128]{2,1,0:T(8,128)S(1)} %get-tuple-element.15), channel_id=1, source_target_pairs={{0,3},{1,2},{2,1},{3,0},{4,7},{5,6},{6,5},{7,4},{8,11},{9,10},{10,... | collective-permute-start | bytes 49160 | tf_op jit(solution)/shard_map/ppermute | solution.py:277
  28.7 21.8 %collective-permute-start.3 = (f32[4,8,128]{2,1,0:T(8,128)S(1)}, f32[4,8,128]{2,1,0:T(8,128)S(1)}, u32[]{:S(2)}, u32[]{:S(2)}) collective-permute-start(f32[4,8,128]{2,1,0:T(8,128)S(1)} %get-tuple-element.16), channel_id=1, source_target_pairs={{0,4},{1,5},{2,6},{3,7},{4,0},{5,1},{6,2},{7,3},{8,12},{9,13},{10,... | collective-permute-start | bytes 49160 | tf_op jit(solution)/shard_map/ppermute | solution.py:277
  31.2 19.4 %collective-permute-start.4 = (f32[4,8,128]{2,1,0:T(8,128)S(1)}, f32[4,8,128]{2,1,0:T(8,128)S(1)}, u32[]{:S(2)}, u32[]{:S(2)}) collective-permute-start(f32[4,8,128]{2,1,0:T(8,128)S(1)} %get-tuple-element.17), channel_id=1, source_target_pairs={{0,5},{1,4},{2,7},{3,6},{4,1},{5,0},{6,3},{7,2},{8,13},{9,12},{10,... | collective-permute-start | bytes 49160 | tf_op jit(solution)/shard_map/ppermute | solution.py:277
  43.4 8.0 %collective-permute-start.5 = (f32[4,8,128]{2,1,0:T(8,128)S(1)}, f32[4,8,128]{2,1,0:T(8,128)S(1)}, u32[]{:S(2)}, u32[]{:S(2)}) collective-permute-start(f32[4,8,128]{2,1,0:T(8,128)S(1)} %get-tuple-element.18), channel_id=1, source_target_pairs={{0,6},{1,7},{2,4},{3,5},{4,2},{5,3},{6,0},{7,1},{8,14},{9,15},{10,... | collective-permute-start | bytes 49160 | tf_op jit(solution)/shard_map/ppermute | solution.py:277
  49.7 7.4 %collective-permute-start.6 = (f32[4,8,128]{2,1,0:T(8,128)S(1)}, f32[4,8,128]{2,1,0:T(8,128)S(1)}, u32[]{:S(2)}, u32[]{:S(2)}) collective-permute-start(f32[4,8,128]{2,1,0:T(8,128)S(1)} %get-tuple-element.19), channel_id=1, source_target_pairs={{0,7},{1,6},{2,5},{3,4},{4,3},{5,2},{6,1},{7,0},{8,15},{9,14},{10,... | collective-permute-start | bytes 49160 | tf_op jit(solution)/shard_map/ppermute | solution.py:277
  59.1 1.3 %collective-permute-start.7 = (f32[2,64,128]{2,1,0:T(8,128)S(1)}, f32[2,64,128]{2,1,0:T(8,128)S(1)}, u32[]{:S(2)}, u32[]{:S(2)}) collective-permute-start(f32[2,64,128]{2,1,0:T(8,128)S(1)} %get-tuple-element.20), channel_id=1, source_target_pairs={{0,8},{8,0},{16,24},{24,16},{32,40},{40,32},{48,56},{56,48},{64,72... | collective-permute-start | bytes 196616 | tf_op jit(solution)/shard_map/ppermute | solution.py:295
  60.5 4.3 %collective-permute-start.8 = (f32[2,64,128]{2,1,0:T(8,128)S(1)}, f32[2,64,128]{2,1,0:T(8,128)S(1)}, u32[]{:S(2)}, u32[]{:S(2)}) collective-permute-start(f32[2,64,128]{2,1,0:T(8,128)S(1)} %add.9), channel_id=1, source_target_pairs={{0,64},{8,72},{16,80},{24,88},{32,96},{40,104},{48,112},{56,120},{... | collective-permute-start | bytes 196616 | tf_op jit(solution)/shard_map/ppermute | solution.py:295
  64.8 4.3 %collective-permute-start.9 = (f32[2,64,128]{2,1,0:T(8,128)S(1)}, f32[2,64,128]{2,1,0:T(8,128)S(1)}, u32[]{:S(2)}, u32[]{:S(2)}) collective-permute-start(f32[2,64,128]{2,1,0:T(8,128)S(1)} %add.10), channel_id=1, source_target_pairs={{0,16},{8,24},{16,0},{24,8},{32,48},{40,56},{48,32},{56,40},{64,80... | collective-permute-start | bytes 196616 | tf_op jit(solution)/shard_map/ppermute | solution.py:295
  69.2 5.7 %collective-permute-start.10 = (f32[2,64,128]{2,1,0:T(8,128)S(1)}, f32[2,64,128]{2,1,0:T(8,128)S(1)}, u32[]{:S(2)}, u32[]{:S(2)}) collective-permute-start(f32[2,64,128]{2,1,0:T(8,128)S(1)} %add.11.refs_0_), channel_id=1, source_target_pairs={{0,48},{8,56},{16,32},{24,40},{32,16},{40,24},{48,0},{56,8},{64,11... | collective-permute-start | bytes 196616 | tf_op jit(solution)/shard_map/ppermute | solution.py:296

commit v4 on v3

--- a/solution.py
+++ b/solution.py
@@ -140,13 +140,20 @@
                     out_ref[q, pl.ds(64 * p + row + 2 * a + 1, 1), :] = odd[a : a + 1]
 
 
+def prepare_kernel(s_ref, out_ref):
+    half = s_ref.shape[0] // 2
+    for step in range(2):
+        even, odd = (s_ref[pl.ds(half * step + p, half // 2, stride=2), :] for p in range(2))
+        high, low = split(jnp.transpose(jnp.concatenate([even, odd], axis=1)))
+        out_ref[step, :128] = high
+        out_ref[step, 128:] = low
+
+
 def sketch_kernel(r_ref, d_ref, s_ref, gram_ref, z_ref, acc_ref):
     step = pl.program_id(0)
     depth = r_ref.shape[0] // 8
-    s_even = s_ref[pl.ds(0, depth, stride=2), :]
-    s_odd = s_ref[pl.ds(1, depth, stride=2), :]
-    s_high, s_low = split(jnp.transpose(jnp.concatenate([s_even, s_odd], axis=1)))
-    s_both = jnp.concatenate([s_high, s_low], axis=0)
+    s_both = s_ref[0]
+    s_high = s_both[:128]
 
     @pl.when(step == 0)
     def _():
@@ -161,6 +168,10 @@
     @pl.when(step == pl.num_programs(0) - 1)
     def _():
         low_half = low_lanes((64, 128))
+        squares = []
+        diagonals = []
+        row = lax.broadcasted_iota(jnp.int32, (64, 128), 0)
+        lane = lax.broadcasted_iota(jnp.int32, (64, 128), 1)
         for q in range(2):
             halves = []
             for f in range(2):
@@ -179,7 +190,15 @@
             gram = lax.dot_general(
                 z, z, (((0,), (0,)), ((), ())), precision=lax.Precision.HIGHEST, preferred_element_type=F32
             )
-            gram_ref[q] = jnp.where(low_half, gram[:64], gram[64:])
+            lower, upper = gram[:64], gram[64:]
+            if q == 0:
+                upper = pltpu.roll(upper, 64, 1)
+            else:
+                lower = pltpu.roll(lower, 64, 1)
+            squares.append(jnp.where(lane - 64 * q <= row, lower, upper))
+            diagonals.append(jnp.sum(jnp.where(lane - 64 * q == row, upper, 0.0), axis=0, keepdims=True))
+        gram_ref[:64] = jnp.where(low_half, squares[0], squares[1])
+        gram_ref[64:] = jnp.where(low_lanes((8, 128)), *(jnp.broadcast_to(d, (8, 128)) for d in diagonals))
 
 
 def factor_kernel(scaling, g_ref, h_ref, z_ref, basis_ref, r_ref, u_ref, l_ref):
@@ -187,7 +206,23 @@
     sub = lax.broadcasted_iota(jnp.int32, (8, 128), 0)
     base = lane - lane % 64
     inner = lane % 64
-    g = [[g_ref[q, 8 * b : 8 * b + 8, :] + h_ref[q, 8 * b : 8 * b + 8, :] for b in range(8)] for q in range(2)]
+    low_half = low_lanes((64, 128))
+    packed = g_ref[...] + h_ref[...]
+    square, diagonal = packed[:64], packed[64:65]
+    turned = pltpu.roll(square, 64, 1)
+    squares = jnp.where(low_half, square, turned), jnp.where(low_half, turned, square)
+    flipped = jnp.transpose(jnp.concatenate(squares, axis=0))[:64]
+    turned = pltpu.roll(flipped, 64, 1)
+    flips = jnp.where(low_half, flipped, turned), jnp.where(low_half, turned, flipped)
+    diagonals = pltpu.roll(packed[64:], 64, 1)[:1], diagonal
+    row = lax.broadcasted_iota(jnp.int32, (64, 128), 0)
+    column = lax.broadcasted_iota(jnp.int32, (64, 128), 1) % 64
+    kept = jnp.logical_xor(column > row, low_half)
+    g = []
+    for q in range(2):
+        full = jnp.where(kept, squares[q], flips[q])
+        full = jnp.where(jnp.logical_and(column == row, jnp.logical_not(low_half)), diagonals[q], full)
+        g.append([full[8 * b : 8 * b + 8] for b in range(8)])
     e = [[jnp.where(inner == sub + 8 * b, 1.0, 0.0).astype(F32) for b in range(8)] for _ in range(2)]
 
     def spread(x, row):
@@ -217,7 +252,6 @@
                 for b in range(top, 8):
                     g[q][b] = g[q][b] - mult[b - top] * grow
                     e[q][b] = e[q][b] - mult[b - top] * erow
-    low_half = low_lanes((64, 128))
     for q in range(2):
         u = u_ref[q] * (1.0 / scaling)
         r_ref[2 * q] = u[:, :64]
@@ -271,6 +305,9 @@
         name="own",
         **small(8),
     )
+    prepared = pl.pallas_call(
+        prepare_kernel, out_shape=sd((2, 256, receivers // 4), BF16), name="prepare", **small(8)
+    )(sketch)
     pieces = list(own(pltpu.with_memory_space_constraint(spec, pltpu.HBM), sketch.T))
     for slot in range(1, rcv_count):
         pairs = [(r, r ^ slot) for r in range(rcv_count)]
@@ -282,18 +319,18 @@
         in_specs=[
             pl.BlockSpec((devices * 16, 128), lambda g: (g, 0)),
             pl.BlockSpec((2, 128, 128), lambda g: (0, 0, 0)),
-            pl.BlockSpec((receivers // 2, RANK), lambda g: (g, 0)),
+            pl.BlockSpec((1, 256, receivers // 4), lambda g: (g, 0, 0)),
         ],
-        out_specs=[pl.BlockSpec((2, 64, 128), lambda g: (0, 0, 0)), pl.BlockSpec((2, 128, 128), lambda g: (0, 0, 0))],
-        out_shape=[sd((2, 64, 128), F32), sd((2, 128, 128), F32)],
+        out_specs=[pl.BlockSpec((72, 128), lambda g: (0, 0)), pl.BlockSpec((2, 128, 128), lambda g: (0, 0, 0))],
+        out_shape=[sd((72, 128), F32), sd((2, 128, 128), F32)],
         scratch_shapes=[pltpu.VMEM((4, 128, 256), F32)],
         name="sketch",
         **small(12),
-    )(pltpu.with_memory_space_constraint(received.reshape(devices * 32, 128), pltpu.VMEM), direct, sketch)
+    )(pltpu.with_memory_space_constraint(received.reshape(devices * 32, 128), pltpu.VMEM), direct, prepared)
     src = lax.axis_size("src")
-    for bits in (1, 8, 2):
+    for bits in (1, 9, 3):
         gram = gram + lax.ppermute(gram, "src", [(s, s ^ bits) for s in range(src)])
-    other = lax.ppermute(gram, "src", [(s, s ^ 6) for s in range(src)])
+    other = lax.ppermute(gram, "src", [(s, s ^ 7) for s in range(src)])
     scaling = math.sqrt(2.0 * receivers)
     basis, r_factor = pl.pallas_call(
         lambda *refs: factor_kernel(scaling, *refs),

time: 78.3 us -> 76.5 us (0.977); the launches traced: 78.1 us -> 75.1 us
  waiting for transfers between devices: 25.5 us -> 23.5 us
  starting transfers between devices: 34.6 us -> 33.6 us
    ppermute x3, waiting for transfers between devices: 7.48 us -> 6.24 us  [local(): gram = gram + lax.ppermute(gram, 'src', [(s, s ^ bits) for s in range(src)])]
  transfers between devices with their start and end apart: 12 -> 12, of which waited for: 7 -> 7; matrix products, arithmetic and copies ran while one was open for 0% -> 0% of each run, Pallas kernels for 3% -> 4%
where the time goes in v4:
time: 76.5 us; the launch traced here: 75.1 us
  starting transfers between devices  33.6 us (44%)
  waiting for transfers between devices  23.5 us (31%)
  Pallas kernels  17 us (22%)
    ppermute x7, starting transfers between devices, local(): pieces[slot] = lax.ppermute(pieces[slot], 'rcv', pairs)  17.4 us
    ppermute x7, waiting for transfers between devices, local(): pieces[slot] = lax.ppermute(pieces[slot], 'rcv', pairs)  15.6 us
    all_to_all x1, starting transfers between devices, local(): lax.all_to_all(spec.reshape(devices, 32, 128), ('src', 'rcv'), split_axis...  11.2 us
    pallas_call x1, Pallas kernels, local(): pl.pallas_call(dft_kernel, in_specs=[pl.BlockSpec(memory_space=pltpu.HBM)...  9.38 us
    ppermute x3, waiting for transfers between devices, local(): gram = gram + lax.ppermute(gram, 'src', [(s, s ^ bits) for s in range(src)])  6.24 us
    pallas_call x1, Pallas kernels, local(): pl.pallas_call(lambda *refs: factor_kernel(scaling, *refs), out_shape=[sd...  3.24 us
    ppermute x1, starting transfers between devices, local(): other = lax.ppermute(gram, 'src', [(s, s ^ 7) for s in range(src)])  3.15 us
    pallas_call x1, Pallas kernels, local(): own(pltpu.with_memory_space_constraint(spec, pltpu.HBM), sketch.T)  2.41 us
  transfers between devices with their start and end apart: 12, of which 7 were waited for; matrix products, arithmetic and copies ran while one was open for 0% of the time, Pallas kernels for 4%

profile of v4, /device:TPU:0, one launch (start us, length us, event | category | flops | bytes accessed | tf_op | source)
XLA Modules:
  0.0 75.1 jit_solution(12115349622074858557)
XLA Ops:
  0.6 9.4 %dft.1.spec_ref = f32[128,4,8,128]{3,2,1,0:T(8,128)} custom-call(f32[8,1024,512]{2,1,0:T(8,128)} %x_hbm.1, bf16[128,512]{1,0:T(8,128)(2,1)} %constant.2.clone.w_hbm), custom_call_target="tpu_custom_call" | custom-call | flops 1610612736 | bytes 19922944 | tf_op jit(solution)/shard_map/dft/pallas_call | solution.py:277
  10.0 0.0 copy-start
  10.0 11.2 %all-to-all-start = ((f32[128,32,128]{2,1,0:T(8,128)}), f32[128,32,128]{2,1,0:T(8,128)S(1)}, u32[]{:S(2)}, u32[]{:S(2)}) async-start(f32[128,32,128]{2,1,0:T(8,128)} %bitcast.5), calls=%async_computation | async-start | bytes 4194304 | tf_op jit(solution)/shard_map/all_to_all | solution.py:293
  21.2 0.0 copy-done
  21.2 2.4 %own.1 = (f32[4,8,128]{2,1,0:T(8,128)S(1)}, f32[4,8,128]{2,1,0:T(8,128)S(1)}, f32[4,8,128]{2,1,0:T(8,128)S(1)}, f32[4,8,128]{2,1,0:T(8,128)S(1)}, f32[4,8,128]{2...) custom-call(f32[128,4,8,128]{3,2,1,0:T(8,128)} %dft.1.spec_ref, ...), custom_call_target="tpu_custom_call" | custom-call | flops 3221225472 | bytes 4194304 | tf_op jit(solution)/shard_map/own/pallas_call | solution.py:311
  23.6 2.6 %collective-permute-start = (f32[4,8,128]{2,1,0:T(8,128)S(1)}, f32[4,8,128]{2,1,0:T(8,128)S(1)}, u32[]{:S(2)}, u32[]{:S(2)}) collective-permute-start(f32[4,8,128]{2,1,0:T(8,128)S(1)} %get-tuple-element.13), channel_id=1, source_target_pairs={{0,1},{1,0},{2,3},{3,2},{4,5},{5,4},{6,7},{7,6},{8,9},{9,8},{10,11... | collective-permute-start | bytes 49160 | tf_op jit(solution)/shard_map/ppermute | solution.py:314
  26.2 1.5 %collective-permute-start.1 = (f32[4,8,128]{2,1,0:T(8,128)S(1)}, f32[4,8,128]{2,1,0:T(8,128)S(1)}, u32[]{:S(2)}, u32[]{:S(2)}) collective-permute-start(f32[4,8,128]{2,1,0:T(8,128)S(1)} %get-tuple-element.14), channel_id=1, source_target_pairs={{0,2},{1,3},{2,0},{3,1},{4,6},{5,7},{6,4},{7,5},{8,10},{9,11},{10,... | collective-permute-start | bytes 49160 | tf_op jit(solution)/shard_map/ppermute | solution.py:314
  27.7 1.1 %collective-permute-start.2 = (f32[4,8,128]{2,1,0:T(8,128)S(1)}, f32[4,8,128]{2,1,0:T(8,128)S(1)}, u32[]{:S(2)}, u32[]{:S(2)}) collective-permute-start(f32[4,8,128]{2,1,0:T(8,128)S(1)} %get-tuple-element.15), channel_id=1, source_target_pairs={{0,3},{1,2},{2,1},{3,0},{4,7},{5,6},{6,5},{7,4},{8,11},{9,10},{10,... | collective-permute-start | bytes 49160 | tf_op jit(solution)/shard_map/ppermute | solution.py:314
  28.7 2.5 %collective-permute-start.3 = (f32[4,8,128]{2,1,0:T(8,128)S(1)}, f32[4,8,128]{2,1,0:T(8,128)S(1)}, u32[]{:S(2)}, u32[]{:S(2)}) collective-permute-start(f32[4,8,128]{2,1,0:T(8,128)S(1)} %get-tuple-element.16), channel_id=1, source_target_pairs={{0,4},{1,5},{2,6},{3,7},{4,0},{5,1},{6,2},{7,3},{8,12},{9,13},{10,... | collective-permute-start | bytes 49160 | tf_op jit(solution)/shard_map/ppermute | solution.py:314
  31.2 3.0 %collective-permute-start.4 = (f32[4,8,128]{2,1,0:T(8,128)S(1)}, f32[4,8,128]{2,1,0:T(8,128)S(1)}, u32[]{:S(2)}, u32[]{:S(2)}) collective-permute-start(f32[4,8,128]{2,1,0:T(8,128)S(1)} %get-tuple-element.17), channel_id=1, source_target_pairs={{0,5},{1,4},{2,7},{3,6},{4,1},{5,0},{6,3},{7,2},{8,13},{9,12},{10,... | collective-permute-start | bytes 49160 | tf_op jit(solution)/shard_map/ppermute | solution.py:314
  34.2 9.2 %collective-permute-done.refs_1_ = f32[4,8,128]{2,1,0:T(8,128)S(1)} collective-permute-done((f32[4,8,128]{2,1,0:T(8,128)S(1)}, f32[4,8,128]{2,1,0:T(8,128)S(1)}, u32[]{:S(2)}, u32[]{:S(2)}) %collective-permute-start) | collective-permute-done | bytes 16416 | tf_op jit(solution)/shard_map/ppermute | solution.py:314
  43.4 6.3 %collective-permute-start.5 = (f32[4,8,128]{2,1,0:T(8,128)S(1)}, f32[4,8,128]{2,1,0:T(8,128)S(1)}, u32[]{:S(2)}, u32[]{:S(2)}) collective-permute-start(f32[4,8,128]{2,1,0:T(8,128)S(1)} %get-tuple-element.18), channel_id=1, source_target_pairs={{0,6},{1,7},{2,4},{3,5},{4,2},{5,3},{6,0},{7,1},{8,14},{9,15},{10,... | collective-permute-start | bytes 49160 | tf_op jit(solution)/shard_map/ppermute | solution.py:314
  49.7 0.0 collective-permute-done.1.refs_2_
  49.7 0.6 collective-permute-start.6
  50.3 0.2 copy.5.s_ref
  50.5 0.2 prepare.1.s_ref
  50.8 0.0 collective-permute-done.2.refs_3_
  50.8 0.0 collective-permute-done.3.refs_4_
  50.8 0.0 collective-permute-done.4.refs_5_
  50.8 0.7 collective-permute-done.5.refs_6_
  51.4 5.6 %collective-permute-done.6.refs_7_ = f32[4,8,128]{2,1,0:T(8,128)S(1)} collective-permute-done((f32[4,8,128]{2,1,0:T(8,128)S(1)}, f32[4,8,128]{2,1,0:T(8,128)S(1)}, u32[]{:S(2)}, u32[]{:S(2)}) %collective-permute-start.6) | collective-permute-done | bytes 16416 | tf_op jit(solution)/shard_map/ppermute | solution.py:314
  57.1 0.1 place.1.d_ref
  57.2 0.0 all-to-all-done
  57.2 1.6 %sketch.1 = (f32[72,128]{1,0:T(8,128)S(1)}, f32[2,128,128]{2,1,0:T(8,128)S(1)}) custom-call(f32[4096,128]{1,0:T(8,128)S(1)} %bitcast.3, f32[2,128,128]{2,1,0:T(8,128)S(1)} %place.1.d_ref, bf16[2,256,256]{2,1,0:T(8,128)(2,1)S(1)} %prepare.1.s_ref), custom_call_target="tpu_custom_call" | custom-call | tf_op jit(solution)/shard_map/sketch/pallas_call | solution.py:316
  58.8 0.1 collective-permute-start.7
  58.9 1.2 %collective-permute-done.7 = f32[72,128]{1,0:T(8,128)S(1)} collective-permute-done((f32[72,128]{1,0:T(8,128)S(1)}, f32[72,128]{1,0:T(8,128)S(1)}, u32[]{:S(2)}, u32[]{:S(2)}) %collective-permute-start.7) | collective-permute-done | bytes 36896 | tf_op jit(solution)/shard_map/ppermute | solution.py:332
  60.1 0.4 collective-permute-start.8
  60.5 3.1 %collective-permute-done.8 = f32[72,128]{1,0:T(8,128)S(1)} collective-permute-done((f32[72,128]{1,0:T(8,128)S(1)}, f32[72,128]{1,0:T(8,128)S(1)}, u32[]{:S(2)}, u32[]{:S(2)}) %collective-permute-start.8) | collective-permute-done | bytes 36896 | tf_op jit(solution)/shard_map/ppermute | solution.py:332
  63.6 1.5 %collective-permute-start.9 = (f32[72,128]{1,0:T(8,128)S(1)}, f32[72,128]{1,0:T(8,128)S(1)}, u32[]{:S(2)}, u32[]{:S(2)}) collective-permute-start(f32[72,128]{1,0:T(8,128)S(1)} %add.10), channel_id=1, source_target_pairs={{0,24},{8,16},{16,8},{24,0},{32,56},{40,48},{48,40},{56,32},{64,88... | collective-permute-start | bytes 110600 | tf_op jit(solution)/shard_map/ppermute | solution.py:332
  65.0 2.0 %collective-permute-done.9 = f32[72,128]{1,0:T(8,128)S(1)} collective-permute-done((f32[72,128]{1,0:T(8,128)S(1)}, f32[72,128]{1,0:T(8,128)S(1)}, u32[]{:S(2)}, u32[]{:S(2)}) %collective-permute-start.9) | collective-permute-done | bytes 36896 | tf_op jit(solution)/shard_map/ppermute | solution.py:332
  67.0 3.2 %collective-permute-start.10 = (f32[72,128]{1,0:T(8,128)S(1)}, f32[72,128]{1,0:T(8,128)S(1)}, u32[]{:S(2)}, u32[]{:S(2)}) collective-permute-start(f32[72,128]{1,0:T(8,128)S(1)} %add.11.refs_0_), channel_id=1, source_target_pairs={{0,56},{8,48},{16,40},{24,32},{32,24},{40,16},{48,8},{56,0},{64,12... | collective-permute-start | bytes 110600 | tf_op jit(solution)/shard_map/ppermute | solution.py:333
  70.2 1.6 %collective-permute-done.10.refs_1_ = f32[72,128]{1,0:T(8,128)S(1)} collective-permute-done((f32[72,128]{1,0:T(8,128)S(1)}, f32[72,128]{1,0:T(8,128)S(1)}, u32[]{:S(2)}, u32[]{:S(2)}) %collective-permute-start.10) | collective-permute-done | bytes 36896 | tf_op jit(solution)/shard_map/ppermute | solution.py:333
  71.8 3.2 %factor.1 = (f32[4,2,64,64]{3,2,1,0:T(8,128)}, f32[4,64,64]{2,1,0:T(8,128)}) custom-call(f32[72,128]{1,0:T(8,128)S(1)} %add.11.refs_0_, f32[72,128]{1,0:T(8,128)S(1)} %collective-permute-done.10.refs_1_, f32[2,128,128]{2,1,0:T(8,128)S(1)} %get-tuple-element.21.refs_2_), custom_call_target="tpu_custom_call" | custom-call | tf_op jit(solution)/shard_map/factor/pallas_call | solution.py:335
  (3 shorter events, 0.0 us)
Async XLA Ops:
  10.0 11.2 %copy-start = (f32[1024,64]{0,1:T(8,128)S(1)}, f32[1024,64]{0,1:T(8,128)}, u32[]{:S(2)}) copy-start(f32[1024,64]{0,1:T(8,128)} %param.4) | copy-start | bytes 786436
  10.0 47.2 %all-to-all-start = ((f32[128,32,128]{2,1,0:T(8,128)}), f32[128,32,128]{2,1,0:T(8,128)S(1)}, u32[]{:S(2)}, u32[]{:S(2)}) async-start(f32[128,32,128]{2,1,0:T(8,128)} %bitcast.5), calls=%async_computation | async-start | bytes 4194304 | tf_op jit(solution)/shard_map/all_to_all | solution.py:293
  23.6 19.8 %collective-permute-start = (f32[4,8,128]{2,1,0:T(8,128)S(1)}, f32[4,8,128]{2,1,0:T(8,128)S(1)}, u32[]{:S(2)}, u32[]{:S(2)}) collective-permute-start(f32[4,8,128]{2,1,0:T(8,128)S(1)} %get-tuple-element.13), channel_id=1, source_target_pairs={{0,1},{1,0},{2,3},{3,2},{4,5},{5,4},{6,7},{7,6},{8,9},{9,8},{10,11... | collective-permute-start | bytes 49160 | tf_op jit(solution)/shard_map/ppermute | solution.py:314
  26.2 23.5 %collective-permute-start.1 = (f32[4,8,128]{2,1,0:T(8,128)S(1)}, f32[4,8,128]{2,1,0:T(8,128)S(1)}, u32[]{:S(2)}, u32[]{:S(2)}) collective-permute-start(f32[4,8,128]{2,1,0:T(8,128)S(1)} %get-tuple-element.14), channel_id=1, source_target_pairs={{0,2},{1,3},{2,0},{3,1},{4,6},{5,7},{6,4},{7,5},{8,10},{9,11},{10,... | collective-permute-start | bytes 49160 | tf_op jit(solution)/shard_map/ppermute | solution.py:314
  27.7 23.1 %collective-permute-start.2 = (f32[4,8,128]{2,1,0:T(8,128)S(1)}, f32[4,8,128]{2,1,0:T(8,128)S(1)}, u32[]{:S(2)}, u32[]{:S(2)}) collective-permute-start(f32[4,8,128]{2,1,0:T(8,128)S(1)} %get-tuple-element.15), channel_id=1, source_target_pairs={{0,3},{1,2},{2,1},{3,0},{4,7},{5,6},{6,5},{7,4},{8,11},{9,10},{10,... | collective-permute-start | bytes 49160 | tf_op jit(solution)/shard_map/ppermute | solution.py:314
  28.7 22.1 %collective-permute-start.3 = (f32[4,8,128]{2,1,0:T(8,128)S(1)}, f32[4,8,128]{2,1,0:T(8,128)S(1)}, u32[]{:S(2)}, u32[]{:S(2)}) collective-permute-start(f32[4,8,128]{2,1,0:T(8,128)S(1)} %get-tuple-element.16), channel_id=1, source_target_pairs={{0,4},{1,5},{2,6},{3,7},{4,0},{5,1},{6,2},{7,3},{8,12},{9,13},{10,... | collective-permute-start | bytes 49160 | tf_op jit(solution)/shard_map/ppermute | solution.py:314
  31.2 19.6 %collective-permute-start.4 = (f32[4,8,128]{2,1,0:T(8,128)S(1)}, f32[4,8,128]{2,1,0:T(8,128)S(1)}, u32[]{:S(2)}, u32[]{:S(2)}) collective-permute-start(f32[4,8,128]{2,1,0:T(8,128)S(1)} %get-tuple-element.17), channel_id=1, source_target_pairs={{0,5},{1,4},{2,7},{3,6},{4,1},{5,0},{6,3},{7,2},{8,13},{9,12},{10,... | collective-permute-start | bytes 49160 | tf_op jit(solution)/shard_map/ppermute | solution.py:314
  43.4 8.0 %collective-permute-start.5 = (f32[4,8,128]{2,1,0:T(8,128)S(1)}, f32[4,8,128]{2,1,0:T(8,128)S(1)}, u32[]{:S(2)}, u32[]{:S(2)}) collective-permute-start(f32[4,8,128]{2,1,0:T(8,128)S(1)} %get-tuple-element.18), channel_id=1, source_target_pairs={{0,6},{1,7},{2,4},{3,5},{4,2},{5,3},{6,0},{7,1},{8,14},{9,15},{10,... | collective-permute-start | bytes 49160 | tf_op jit(solution)/shard_map/ppermute | solution.py:314
  49.7 7.4 %collective-permute-start.6 = (f32[4,8,128]{2,1,0:T(8,128)S(1)}, f32[4,8,128]{2,1,0:T(8,128)S(1)}, u32[]{:S(2)}, u32[]{:S(2)}) collective-permute-start(f32[4,8,128]{2,1,0:T(8,128)S(1)} %get-tuple-element.19), channel_id=1, source_target_pairs={{0,7},{1,6},{2,5},{3,4},{4,3},{5,2},{6,1},{7,0},{8,15},{9,14},{10,... | collective-permute-start | bytes 49160 | tf_op jit(solution)/shard_map/ppermute | solution.py:314
  58.8 1.3 %collective-permute-start.7 = (f32[72,128]{1,0:T(8,128)S(1)}, f32[72,128]{1,0:T(8,128)S(1)}, u32[]{:S(2)}, u32[]{:S(2)}) collective-permute-start(f32[72,128]{1,0:T(8,128)S(1)} %get-tuple-element.20), channel_id=1, source_target_pairs={{0,8},{8,0},{16,24},{24,16},{32,40},{40,32},{48,56},{56,48},{64,72... | collective-permute-start | bytes 110600 | tf_op jit(solution)/shard_map/ppermute | solution.py:332
  60.1 3.4 %collective-permute-start.8 = (f32[72,128]{1,0:T(8,128)S(1)}, f32[72,128]{1,0:T(8,128)S(1)}, u32[]{:S(2)}, u32[]{:S(2)}) collective-permute-start(f32[72,128]{1,0:T(8,128)S(1)} %add.9), channel_id=1, source_target_pairs={{0,72},{8,64},{16,88},{24,80},{32,104},{40,96},{48,120},{56,112},{... | collective-permute-start | bytes 110600 | tf_op jit(solution)/shard_map/ppermute | solution.py:332
  63.6 3.4 %collective-permute-start.9 = (f32[72,128]{1,0:T(8,128)S(1)}, f32[72,128]{1,0:T(8,128)S(1)}, u32[]{:S(2)}, u32[]{:S(2)}) collective-permute-start(f32[72,128]{1,0:T(8,128)S(1)} %add.10), channel_id=1, source_target_pairs={{0,24},{8,16},{16,8},{24,0},{32,56},{40,48},{48,40},{56,32},{64,88... | collective-permute-start | bytes 110600 | tf_op jit(solution)/shard_map/ppermute | solution.py:332
  67.0 4.8 %collective-permute-start.10 = (f32[72,128]{1,0:T(8,128)S(1)}, f32[72,128]{1,0:T(8,128)S(1)}, u32[]{:S(2)}, u32[]{:S(2)}) collective-permute-start(f32[72,128]{1,0:T(8,128)S(1)} %add.11.refs_0_), channel_id=1, source_target_pairs={{0,56},{8,48},{16,40},{24,32},{32,24},{40,16},{48,8},{56,0},{64,12... | collective-permute-start | bytes 110600 | tf_op jit(solution)/shard_map/ppermute | solution.py:333

commit v5 on v4

--- a/solution.py
+++ b/solution.py
@@ -42,16 +42,19 @@
     return lax.broadcasted_iota(jnp.int32, shape, 1) < 64
 
 
+SPANS = (2, 4, 4, 4, 2)
+
+
 def dft_kernel(x_hbm, w_hbm, spec_hbm, x_ref, w_ref, out_ref, x_sems, w_sem, out_sems):
-    steps = x_ref.shape[1] // 128
-    ahead = 3
+    starts = [sum(SPANS[:k]) for k in range(len(SPANS))]
+    ahead = 2
 
     def fetch(step):
-        span = pl.ds(pl.multiple_of(128 * step, 128), 128)
+        span = pl.ds(64 * starts[step], 64 * SPANS[step])
         return pltpu.make_async_copy(x_hbm.at[:, span, :], x_ref.at[:, span, :], x_sems.at[step])
 
     def put(step):
-        span = pl.ds(pl.multiple_of(16 * step, 16), 16)
+        span = pl.ds(8 * starts[step], 8 * SPANS[step])
         return pltpu.make_async_copy(out_ref.at[span], spec_hbm.at[span], out_sems.at[step])
 
     w_copy = pltpu.make_async_copy(w_hbm, w_ref, w_sem)
@@ -59,29 +62,22 @@
     for step in range(ahead):
         fetch(step).start()
     w_copy.wait()
-
-    def body(step, carry):
+    for step in range(len(SPANS)):
         fetch(step).wait()
-
-        @pl.when(step + ahead < steps)
-        def _():
+        if step + ahead < len(SPANS):
             fetch(step + ahead).start()
-
         weights = w_ref[...]
-        for tile in range(2):
-            rows = pl.ds(pl.multiple_of(128 * step + 64 * tile, 64), 64)
-            dest = pl.ds(pl.multiple_of(16 * step + 8 * tile, 8), 8)
+        for tile in range(starts[step], starts[step] + SPANS[step]):
             for half in range(2):
-                high, low = split(x_ref[4 * half : 4 * half + 4, rows, :].reshape(256, -1))
+                x = x_ref[4 * half : 4 * half + 4, 64 * tile : 64 * tile + 64, :]
+                high, low = split(x.reshape(256, -1))
                 both = mm(weights, high, NT)
                 out = both[:64] + both[64:] + mm(weights[:64], low, NT)
                 for c in range(2):
-                    out_ref[dest, 2 * half + c] = out[:, 128 * c : 128 * c + 128].reshape(8, 8, 128)
+                    piece = out[:, 128 * c : 128 * c + 128]
+                    out_ref[8 * tile : 8 * tile + 8, 2 * half + c] = piece.reshape(8, 8, 128)
         put(step).start()
-        return carry
-
-    lax.fori_loop(0, steps, body, 0)
-    for step in range(steps):
+    for step in range(len(SPANS)):
         put(step).wait()
 
 
@@ -141,64 +137,53 @@
 
 
 def prepare_kernel(s_ref, out_ref):
-    half = s_ref.shape[0] // 2
-    for step in range(2):
-        even, odd = (s_ref[pl.ds(half * step + p, half // 2, stride=2), :] for p in range(2))
-        high, low = split(jnp.transpose(jnp.concatenate([even, odd], axis=1)))
-        out_ref[step, :128] = high
-        out_ref[step, 128:] = low
-
-
-def sketch_kernel(r_ref, d_ref, s_ref, gram_ref, z_ref, acc_ref):
-    step = pl.program_id(0)
+    even, odd = (s_ref[pl.ds(p, s_ref.shape[0] // 2, stride=2), :] for p in range(2))
+    high, low = split(jnp.transpose(jnp.concatenate([even, odd], axis=1)))
+    out_ref[:128] = high
+    out_ref[128:] = low
+
+
+def sketch_kernel(r_ref, d_ref, s_ref, gram_ref, z_ref):
     depth = r_ref.shape[0] // 8
-    s_both = s_ref[0]
+    s_both = s_ref[...]
     s_high = s_both[:128]
-
-    @pl.when(step == 0)
-    def _():
-        acc_ref[...] = jnp.zeros_like(acc_ref)
-
+    sums = []
     for pair in range(4):
         block = jnp.concatenate([r_ref[pl.ds(2 * pair + p, depth, stride=8), :] for p in range(2)], axis=1)
         high, low = split(block)
         both = mm(s_both, high, NN)
-        acc_ref[pair] += both[:128] + both[128:] + mm(s_high, low, NN)
-
-    @pl.when(step == pl.num_programs(0) - 1)
-    def _():
-        low_half = low_lanes((64, 128))
-        squares = []
-        diagonals = []
-        row = lax.broadcasted_iota(jnp.int32, (64, 128), 0)
-        lane = lax.broadcasted_iota(jnp.int32, (64, 128), 1)
-        for q in range(2):
-            halves = []
-            for f in range(2):
-                sums = acc_ref[2 * q + f]
-                x, y = sums[:, :128], sums[:, 128:]
-                halves.append(
-                    jnp.where(
-                        low_half,
-                        x[:64] + pltpu.roll(x[64:], 64, 1),
-                        pltpu.roll(y[:64], 64, 1) + y[64:],
-                    )
+        sums.append(both[:128] + both[128:] + mm(s_high, low, NN))
+    low_half = low_lanes((64, 128))
+    squares = []
+    diagonals = []
+    row = lax.broadcasted_iota(jnp.int32, (64, 128), 0)
+    lane = lax.broadcasted_iota(jnp.int32, (64, 128), 1)
+    for q in range(2):
+        halves = []
+        for f in range(2):
+            x, y = sums[2 * q + f][:, :128], sums[2 * q + f][:, 128:]
+            halves.append(
+                jnp.where(
+                    low_half,
+                    x[:64] + pltpu.roll(x[64:], 64, 1),
+                    pltpu.roll(y[:64], 64, 1) + y[64:],
                 )
-            reverse = jnp.transpose(jnp.concatenate(halves, axis=0))
-            z = 0.5 * (d_ref[q] + reverse)
-            z_ref[q] = z
-            gram = lax.dot_general(
-                z, z, (((0,), (0,)), ((), ())), precision=lax.Precision.HIGHEST, preferred_element_type=F32
             )
-            lower, upper = gram[:64], gram[64:]
-            if q == 0:
-                upper = pltpu.roll(upper, 64, 1)
-            else:
-                lower = pltpu.roll(lower, 64, 1)
-            squares.append(jnp.where(lane - 64 * q <= row, lower, upper))
-            diagonals.append(jnp.sum(jnp.where(lane - 64 * q == row, upper, 0.0), axis=0, keepdims=True))
-        gram_ref[:64] = jnp.where(low_half, squares[0], squares[1])
-        gram_ref[64:] = jnp.where(low_lanes((8, 128)), *(jnp.broadcast_to(d, (8, 128)) for d in diagonals))
+        reverse = jnp.transpose(jnp.concatenate(halves, axis=0))
+        z = 0.5 * (d_ref[q] + reverse)
+        z_ref[q] = z
+        gram = lax.dot_general(
+            z, z, (((0,), (0,)), ((), ())), precision=lax.Precision.HIGHEST, preferred_element_type=F32
+        )
+        lower, upper = gram[:64], gram[64:]
+        if q == 0:
+            upper = pltpu.roll(upper, 64, 1)
+        else:
+            lower = pltpu.roll(lower, 64, 1)
+        squares.append(jnp.where(lane - 64 * q <= row, lower, upper))
+        diagonals.append(jnp.sum(jnp.where(lane - 64 * q == row, upper, 0.0), axis=0, keepdims=True))
+    gram_ref[:64] = jnp.where(low_half, squares[0], squares[1])
+    gram_ref[64:] = jnp.where(low_lanes((8, 128)), *(jnp.broadcast_to(d, (8, 128)) for d in diagonals))
 
 
 def factor_kernel(scaling, g_ref, h_ref, z_ref, basis_ref, r_ref, u_ref, l_ref):
@@ -283,9 +268,9 @@
             pltpu.VMEM((shots, receivers, samples), F32),
             pltpu.VMEM((128, samples), BF16),
             pltpu.VMEM((devices, 4, 8, 128), F32),
-            pltpu.SemaphoreType.DMA((receivers // 128,)),
+            pltpu.SemaphoreType.DMA((len(SPANS),)),
             pltpu.SemaphoreType.DMA,
-            pltpu.SemaphoreType.DMA((receivers // 128,)),
+            pltpu.SemaphoreType.DMA((len(SPANS),)),
         ],
         cost_estimate=pl.CostEstimate(flops=3 * 2 * 64 * 8192 * 512, bytes_accessed=19 << 20, transcendentals=0),
         name="dft",
@@ -306,7 +291,7 @@
         **small(8),
     )
     prepared = pl.pallas_call(
-        prepare_kernel, out_shape=sd((2, 256, receivers // 4), BF16), name="prepare", **small(8)
+        prepare_kernel, out_shape=sd((256, receivers // 2), BF16), name="prepare", **small(8)
     )(sketch)
     pieces = list(own(pltpu.with_memory_space_constraint(spec, pltpu.HBM), sketch.T))
     for slot in range(1, rcv_count):
@@ -315,15 +300,8 @@
     direct = pl.pallas_call(place_kernel, out_shape=sd((2, 128, 128), F32), name="place", **small(8))(*pieces)
     gram, z = pl.pallas_call(
         sketch_kernel,
-        grid=(2,),
-        in_specs=[
-            pl.BlockSpec((devices * 16, 128), lambda g: (g, 0)),
-            pl.BlockSpec((2, 128, 128), lambda g: (0, 0, 0)),
-            pl.BlockSpec((1, 256, receivers // 4), lambda g: (g, 0, 0)),
-        ],
-        out_specs=[pl.BlockSpec((72, 128), lambda g: (0, 0)), pl.BlockSpec((2, 128, 128), lambda g: (0, 0, 0))],
+        in_specs=[pl.BlockSpec(memory_space=pltpu.VMEM)] * 3,
         out_shape=[sd((72, 128), F32), sd((2, 128, 128), F32)],
-        scratch_shapes=[pltpu.VMEM((4, 128, 256), F32)],
         name="sketch",
         **small(12),
     )(pltpu.with_memory_space_constraint(received.reshape(devices * 32, 128), pltpu.VMEM), direct, prepared)

time: 76.5 us -> 75.7 us (0.990)
  Pallas kernels: 17 us -> 16.2 us
where the time goes in v5:
time: 75.7 us; the launch traced here: 74.3 us
  starting transfers between devices  33.6 us (44%)
  waiting for transfers between devices  23.5 us (31%)
  Pallas kernels  16.2 us (21%)
    ppermute x7, starting transfers between devices, local(): pieces[slot] = lax.ppermute(pieces[slot], 'rcv', pairs)  17.4 us
    ppermute x7, waiting for transfers between devices, local(): pieces[slot] = lax.ppermute(pieces[slot], 'rcv', pairs)  15.6 us
    all_to_all x1, starting transfers between devices, local(): lax.all_to_all(spec.reshape(devices, 32, 128), ('src', 'rcv'), split_axis...  11.2 us
    pallas_call x1, Pallas kernels, local(): pl.pallas_call(dft_kernel, in_specs=[pl.BlockSpec(memory_space=pltpu.HBM)...  8.92 us
    ppermute x3, waiting for transfers between devices, local(): gram = gram + lax.ppermute(gram, 'src', [(s, s ^ bits) for s in range(src)])  6.24 us
    pallas_call x1, Pallas kernels, local(): pl.pallas_call(lambda *refs: factor_kernel(scaling, *refs), out_shape=[sd...  3.24 us
    ppermute x1, starting transfers between devices, local(): other = lax.ppermute(gram, 'src', [(s, s ^ 7) for s in range(src)])  3.14 us
    pallas_call x1, Pallas kernels, local(): own(pltpu.with_memory_space_constraint(spec, pltpu.HBM), sketch.T)  2.41 us
  transfers between devices with their start and end apart: 12, of which 7 were waited for; matrix products, arithmetic and copies ran while one was open for 0% of the time, Pallas kernels for 4%

profile of v5, /device:TPU:0, one launch (start us, length us, event | category | flops | bytes accessed | tf_op | source)
XLA Modules:
  0.0 74.3 jit_solution(17596756030218429325)
XLA Ops:
  0.6 8.9 %dft.1.spec_ref = f32[128,4,8,128]{3,2,1,0:T(8,128)} custom-call(f32[8,1024,512]{2,1,0:T(8,128)} %x_hbm.1, bf16[128,512]{1,0:T(8,128)(2,1)} %constant.2.clone.w_hbm), custom_call_target="tpu_custom_call" | custom-call | flops 1610612736 | bytes 19922944 | tf_op jit(solution)/shard_map/dft/pallas_call | solution.py:262
  9.6 0.0 copy-start
  9.6 11.2 %all-to-all-start = ((f32[128,32,128]{2,1,0:T(8,128)}), f32[128,32,128]{2,1,0:T(8,128)S(1)}, u32[]{:S(2)}, u32[]{:S(2)}) async-start(f32[128,32,128]{2,1,0:T(8,128)} %bitcast.5), calls=%async_computation | async-start | bytes 4194304 | tf_op jit(solution)/shard_map/all_to_all | solution.py:278
  20.8 0.0 copy-done
  20.8 2.4 %own.1 = (f32[4,8,128]{2,1,0:T(8,128)S(1)}, f32[4,8,128]{2,1,0:T(8,128)S(1)}, f32[4,8,128]{2,1,0:T(8,128)S(1)}, f32[4,8,128]{2,1,0:T(8,128)S(1)}, f32[4,8,128]{2...) custom-call(f32[128,4,8,128]{3,2,1,0:T(8,128)} %dft.1.spec_ref, ...), custom_call_target="tpu_custom_call" | custom-call | flops 3221225472 | bytes 4194304 | tf_op jit(solution)/shard_map/own/pallas_call | solution.py:296
  23.2 2.5 %collective-permute-start = (f32[4,8,128]{2,1,0:T(8,128)S(1)}, f32[4,8,128]{2,1,0:T(8,128)S(1)}, u32[]{:S(2)}, u32[]{:S(2)}) collective-permute-start(f32[4,8,128]{2,1,0:T(8,128)S(1)} %get-tuple-element.13), channel_id=1, source_target_pairs={{0,1},{1,0},{2,3},{3,2},{4,5},{5,4},{6,7},{7,6},{8,9},{9,8},{10,11... | collective-permute-start | bytes 49160 | tf_op jit(solution)/shard_map/ppermute | solution.py:299
  25.7 1.5 %collective-permute-start.1 = (f32[4,8,128]{2,1,0:T(8,128)S(1)}, f32[4,8,128]{2,1,0:T(8,128)S(1)}, u32[]{:S(2)}, u32[]{:S(2)}) collective-permute-start(f32[4,8,128]{2,1,0:T(8,128)S(1)} %get-tuple-element.14), channel_id=1, source_target_pairs={{0,2},{1,3},{2,0},{3,1},{4,6},{5,7},{6,4},{7,5},{8,10},{9,11},{10,... | collective-permute-start | bytes 49160 | tf_op jit(solution)/shard_map/ppermute | solution.py:299
  27.2 1.1 %collective-permute-start.2 = (f32[4,8,128]{2,1,0:T(8,128)S(1)}, f32[4,8,128]{2,1,0:T(8,128)S(1)}, u32[]{:S(2)}, u32[]{:S(2)}) collective-permute-start(f32[4,8,128]{2,1,0:T(8,128)S(1)} %get-tuple-element.15), channel_id=1, source_target_pairs={{0,3},{1,2},{2,1},{3,0},{4,7},{5,6},{6,5},{7,4},{8,11},{9,10},{10,... | collective-permute-start | bytes 49160 | tf_op jit(solution)/shard_map/ppermute | solution.py:299
  28.3 2.5 %collective-permute-start.3 = (f32[4,8,128]{2,1,0:T(8,128)S(1)}, f32[4,8,128]{2,1,0:T(8,128)S(1)}, u32[]{:S(2)}, u32[]{:S(2)}) collective-permute-start(f32[4,8,128]{2,1,0:T(8,128)S(1)} %get-tuple-element.16), channel_id=1, source_target_pairs={{0,4},{1,5},{2,6},{3,7},{4,0},{5,1},{6,2},{7,3},{8,12},{9,13},{10,... | collective-permute-start | bytes 49160 | tf_op jit(solution)/shard_map/ppermute | solution.py:299
  30.7 3.0 %collective-permute-start.4 = (f32[4,8,128]{2,1,0:T(8,128)S(1)}, f32[4,8,128]{2,1,0:T(8,128)S(1)}, u32[]{:S(2)}, u32[]{:S(2)}) collective-permute-start(f32[4,8,128]{2,1,0:T(8,128)S(1)} %get-tuple-element.17), channel_id=1, source_target_pairs={{0,5},{1,4},{2,7},{3,6},{4,1},{5,0},{6,3},{7,2},{8,13},{9,12},{10,... | collective-permute-start | bytes 49160 | tf_op jit(solution)/shard_map/ppermute | solution.py:299
  33.7 9.3 %collective-permute-done.refs_1_ = f32[4,8,128]{2,1,0:T(8,128)S(1)} collective-permute-done((f32[4,8,128]{2,1,0:T(8,128)S(1)}, f32[4,8,128]{2,1,0:T(8,128)S(1)}, u32[]{:S(2)}, u32[]{:S(2)}) %collective-permute-start) | collective-permute-done | bytes 16416 | tf_op jit(solution)/shard_map/ppermute | solution.py:299
  42.9 6.3 %collective-permute-start.5 = (f32[4,8,128]{2,1,0:T(8,128)S(1)}, f32[4,8,128]{2,1,0:T(8,128)S(1)}, u32[]{:S(2)}, u32[]{:S(2)}) collective-permute-start(f32[4,8,128]{2,1,0:T(8,128)S(1)} %get-tuple-element.18), channel_id=1, source_target_pairs={{0,6},{1,7},{2,4},{3,5},{4,2},{5,3},{6,0},{7,1},{8,14},{9,15},{10,... | collective-permute-start | bytes 49160 | tf_op jit(solution)/shard_map/ppermute | solution.py:299
  49.3 0.0 collective-permute-done.1.refs_2_
  49.3 0.6 collective-permute-start.6
  49.9 0.2 copy.5.s_ref
  50.1 0.2 prepare.1.s_ref
  50.3 0.0 collective-permute-done.2.refs_3_
  50.3 0.0 collective-permute-done.3.refs_4_
  50.3 0.0 collective-permute-done.4.refs_5_
  50.3 0.7 collective-permute-done.5.refs_6_
  51.0 5.6 %collective-permute-done.6.refs_7_ = f32[4,8,128]{2,1,0:T(8,128)S(1)} collective-permute-done((f32[4,8,128]{2,1,0:T(8,128)S(1)}, f32[4,8,128]{2,1,0:T(8,128)S(1)}, u32[]{:S(2)}, u32[]{:S(2)}) %collective-permute-start.6) | collective-permute-done | bytes 16416 | tf_op jit(solution)/shard_map/ppermute | solution.py:299
  56.6 0.1 place.1.d_ref
  56.8 0.0 all-to-all-done
  56.8 1.3 %sketch.1 = (f32[72,128]{1,0:T(8,128)S(1)}, f32[2,128,128]{2,1,0:T(8,128)S(1)}) custom-call(f32[4096,128]{1,0:T(8,128)S(1)} %bitcast.3, f32[2,128,128]{2,1,0:T(8,128)S(1)} %place.1.d_ref, bf16[256,512]{1,0:T(8,128)(2,1)S(1)} %prepare.1.s_ref), custom_call_target="tpu_custom_call" | custom-call | tf_op jit(solution)/shard_map/sketch/pallas_call | solution.py:301
  58.1 0.1 collective-permute-start.7
  58.2 1.2 %collective-permute-done.7 = f32[72,128]{1,0:T(8,128)S(1)} collective-permute-done((f32[72,128]{1,0:T(8,128)S(1)}, f32[72,128]{1,0:T(8,128)S(1)}, u32[]{:S(2)}, u32[]{:S(2)}) %collective-permute-start.7) | collective-permute-done | bytes 36896 | tf_op jit(solution)/shard_map/ppermute | solution.py:310
  59.4 0.4 collective-permute-start.8
  59.7 3.1 %collective-permute-done.8 = f32[72,128]{1,0:T(8,128)S(1)} collective-permute-done((f32[72,128]{1,0:T(8,128)S(1)}, f32[72,128]{1,0:T(8,128)S(1)}, u32[]{:S(2)}, u32[]{:S(2)}) %collective-permute-start.8) | collective-permute-done | bytes 36896 | tf_op jit(solution)/shard_map/ppermute | solution.py:310
  62.8 1.5 %collective-permute-start.9 = (f32[72,128]{1,0:T(8,128)S(1)}, f32[72,128]{1,0:T(8,128)S(1)}, u32[]{:S(2)}, u32[]{:S(2)}) collective-permute-start(f32[72,128]{1,0:T(8,128)S(1)} %add.10), channel_id=1, source_target_pairs={{0,24},{8,16},{16,8},{24,0},{32,56},{40,48},{48,40},{56,32},{64,88... | collective-permute-start | bytes 110600 | tf_op jit(solution)/shard_map/ppermute | solution.py:310
  64.3 2.0 %collective-permute-done.9 = f32[72,128]{1,0:T(8,128)S(1)} collective-permute-done((f32[72,128]{1,0:T(8,128)S(1)}, f32[72,128]{1,0:T(8,128)S(1)}, u32[]{:S(2)}, u32[]{:S(2)}) %collective-permute-start.9) | collective-permute-done | bytes 36896 | tf_op jit(solution)/shard_map/ppermute | solution.py:310
  66.3 3.1 %collective-permute-start.10 = (f32[72,128]{1,0:T(8,128)S(1)}, f32[72,128]{1,0:T(8,128)S(1)}, u32[]{:S(2)}, u32[]{:S(2)}) collective-permute-start(f32[72,128]{1,0:T(8,128)S(1)} %add.11.refs_0_), channel_id=1, source_target_pairs={{0,56},{8,48},{16,40},{24,32},{32,24},{40,16},{48,8},{56,0},{64,12... | collective-permute-start | bytes 110600 | tf_op jit(solution)/shard_map/ppermute | solution.py:311
  69.4 1.6 %collective-permute-done.10.refs_1_ = f32[72,128]{1,0:T(8,128)S(1)} collective-permute-done((f32[72,128]{1,0:T(8,128)S(1)}, f32[72,128]{1,0:T(8,128)S(1)}, u32[]{:S(2)}, u32[]{:S(2)}) %collective-permute-start.10) | collective-permute-done | bytes 36896 | tf_op jit(solution)/shard_map/ppermute | solution.py:311
  71.0 3.2 %factor.1 = (f32[4,2,64,64]{3,2,1,0:T(8,128)}, f32[4,64,64]{2,1,0:T(8,128)}) custom-call(f32[72,128]{1,0:T(8,128)S(1)} %add.11.refs_0_, f32[72,128]{1,0:T(8,128)S(1)} %collective-permute-done.10.refs_1_, f32[2,128,128]{2,1,0:T(8,128)S(1)} %get-tuple-element.21.refs_2_), custom_call_target="tpu_custom_call" | custom-call | tf_op jit(solution)/shard_map/factor/pallas_call | solution.py:313
  (3 shorter events, 0.0 us)
Async XLA Ops:
  9.6 11.2 %copy-start = (f32[1024,64]{0,1:T(8,128)S(1)}, f32[1024,64]{0,1:T(8,128)}, u32[]{:S(2)}) copy-start(f32[1024,64]{0,1:T(8,128)} %param.4) | copy-start | bytes 786436
  9.6 47.2 %all-to-all-start = ((f32[128,32,128]{2,1,0:T(8,128)}), f32[128,32,128]{2,1,0:T(8,128)S(1)}, u32[]{:S(2)}, u32[]{:S(2)}) async-start(f32[128,32,128]{2,1,0:T(8,128)} %bitcast.5), calls=%async_computation | async-start | bytes 4194304 | tf_op jit(solution)/shard_map/all_to_all | solution.py:278
  23.2 19.8 %collective-permute-start = (f32[4,8,128]{2,1,0:T(8,128)S(1)}, f32[4,8,128]{2,1,0:T(8,128)S(1)}, u32[]{:S(2)}, u32[]{:S(2)}) collective-permute-start(f32[4,8,128]{2,1,0:T(8,128)S(1)} %get-tuple-element.13), channel_id=1, source_target_pairs={{0,1},{1,0},{2,3},{3,2},{4,5},{5,4},{6,7},{7,6},{8,9},{9,8},{10,11... | collective-permute-start | bytes 49160 | tf_op jit(solution)/shard_map/ppermute | solution.py:299
  25.7 23.5 %collective-permute-start.1 = (f32[4,8,128]{2,1,0:T(8,128)S(1)}, f32[4,8,128]{2,1,0:T(8,128)S(1)}, u32[]{:S(2)}, u32[]{:S(2)}) collective-permute-start(f32[4,8,128]{2,1,0:T(8,128)S(1)} %get-tuple-element.14), channel_id=1, source_target_pairs={{0,2},{1,3},{2,0},{3,1},{4,6},{5,7},{6,4},{7,5},{8,10},{9,11},{10,... | collective-permute-start | bytes 49160 | tf_op jit(solution)/shard_map/ppermute | solution.py:299
  27.2 23.1 %collective-permute-start.2 = (f32[4,8,128]{2,1,0:T(8,128)S(1)}, f32[4,8,128]{2,1,0:T(8,128)S(1)}, u32[]{:S(2)}, u32[]{:S(2)}) collective-permute-start(f32[4,8,128]{2,1,0:T(8,128)S(1)} %get-tuple-element.15), channel_id=1, source_target_pairs={{0,3},{1,2},{2,1},{3,0},{4,7},{5,6},{6,5},{7,4},{8,11},{9,10},{10,... | collective-permute-start | bytes 49160 | tf_op jit(solution)/shard_map/ppermute | solution.py:299
  28.3 22.1 %collective-permute-start.3 = (f32[4,8,128]{2,1,0:T(8,128)S(1)}, f32[4,8,128]{2,1,0:T(8,128)S(1)}, u32[]{:S(2)}, u32[]{:S(2)}) collective-permute-start(f32[4,8,128]{2,1,0:T(8,128)S(1)} %get-tuple-element.16), channel_id=1, source_target_pairs={{0,4},{1,5},{2,6},{3,7},{4,0},{5,1},{6,2},{7,3},{8,12},{9,13},{10,... | collective-permute-start | bytes 49160 | tf_op jit(solution)/shard_map/ppermute | solution.py:299
  30.7 19.6 %collective-permute-start.4 = (f32[4,8,128]{2,1,0:T(8,128)S(1)}, f32[4,8,128]{2,1,0:T(8,128)S(1)}, u32[]{:S(2)}, u32[]{:S(2)}) collective-permute-start(f32[4,8,128]{2,1,0:T(8,128)S(1)} %get-tuple-element.17), channel_id=1, source_target_pairs={{0,5},{1,4},{2,7},{3,6},{4,1},{5,0},{6,3},{7,2},{8,13},{9,12},{10,... | collective-permute-start | bytes 49160 | tf_op jit(solution)/shard_map/ppermute | solution.py:299
  42.9 8.0 %collective-permute-start.5 = (f32[4,8,128]{2,1,0:T(8,128)S(1)}, f32[4,8,128]{2,1,0:T(8,128)S(1)}, u32[]{:S(2)}, u32[]{:S(2)}) collective-permute-start(f32[4,8,128]{2,1,0:T(8,128)S(1)} %get-tuple-element.18), channel_id=1, source_target_pairs={{0,6},{1,7},{2,4},{3,5},{4,2},{5,3},{6,0},{7,1},{8,14},{9,15},{10,... | collective-permute-start | bytes 49160 | tf_op jit(solution)/shard_map/ppermute | solution.py:299
  49.3 7.4 %collective-permute-start.6 = (f32[4,8,128]{2,1,0:T(8,128)S(1)}, f32[4,8,128]{2,1,0:T(8,128)S(1)}, u32[]{:S(2)}, u32[]{:S(2)}) collective-permute-start(f32[4,8,128]{2,1,0:T(8,128)S(1)} %get-tuple-element.19), channel_id=1, source_target_pairs={{0,7},{1,6},{2,5},{3,4},{4,3},{5,2},{6,1},{7,0},{8,15},{9,14},{10,... | collective-permute-start | bytes 49160 | tf_op jit(solution)/shard_map/ppermute | solution.py:299
  58.1 1.3 %collective-permute-start.7 = (f32[72,128]{1,0:T(8,128)S(1)}, f32[72,128]{1,0:T(8,128)S(1)}, u32[]{:S(2)}, u32[]{:S(2)}) collective-permute-start(f32[72,128]{1,0:T(8,128)S(1)} %get-tuple-element.20), channel_id=1, source_target_pairs={{0,8},{8,0},{16,24},{24,16},{32,40},{40,32},{48,56},{56,48},{64,72... | collective-permute-start | bytes 110600 | tf_op jit(solution)/shard_map/ppermute | solution.py:310
  59.4 3.4 %collective-permute-start.8 = (f32[72,128]{1,0:T(8,128)S(1)}, f32[72,128]{1,0:T(8,128)S(1)}, u32[]{:S(2)}, u32[]{:S(2)}) collective-permute-start(f32[72,128]{1,0:T(8,128)S(1)} %add.9), channel_id=1, source_target_pairs={{0,72},{8,64},{16,88},{24,80},{32,104},{40,96},{48,120},{56,112},{... | collective-permute-start | bytes 110600 | tf_op jit(solution)/shard_map/ppermute | solution.py:310
  62.8 3.4 %collective-permute-start.9 = (f32[72,128]{1,0:T(8,128)S(1)}, f32[72,128]{1,0:T(8,128)S(1)}, u32[]{:S(2)}, u32[]{:S(2)}) collective-permute-start(f32[72,128]{1,0:T(8,128)S(1)} %add.10), channel_id=1, source_target_pairs={{0,24},{8,16},{16,8},{24,0},{32,56},{40,48},{48,40},{56,32},{64,88... | collective-permute-start | bytes 110600 | tf_op jit(solution)/shard_map/ppermute | solution.py:310
  66.3 4.8 %collective-permute-start.10 = (f32[72,128]{1,0:T(8,128)S(1)}, f32[72,128]{1,0:T(8,128)S(1)}, u32[]{:S(2)}, u32[]{:S(2)}) collective-permute-start(f32[72,128]{1,0:T(8,128)S(1)} %add.11.refs_0_), channel_id=1, source_target_pairs={{0,56},{8,48},{16,40},{24,32},{32,24},{40,16},{48,8},{56,0},{64,12... | collective-permute-start | bytes 110600 | tf_op jit(solution)/shard_map/ppermute | solution.py:311

commit v6 on v5

--- a/solution.py
+++ b/solution.py
@@ -278,10 +278,10 @@
     received = lax.all_to_all(spec.reshape(devices, 32, 128), ("src", "rcv"), split_axis=0, concat_axis=0, tiled=True)
     own = pl.pallas_call(
         own_kernel,
-        grid=(2,),
+        grid=(4,),
         in_specs=[
-            pl.BlockSpec((devices // 2, 4, 8, 128), lambda g: (g, 0, 0, 0)),
-            pl.BlockSpec((RANK, receivers // 2), lambda g: (0, g)),
+            pl.BlockSpec((devices // 4, 4, 8, 128), lambda g: (g, 0, 0, 0)),
+            pl.BlockSpec((RANK, receivers // 4), lambda g: (0, g)),
         ],
         out_specs=[pl.BlockSpec((4, 8, 128), lambda g: (0, 0, 0))] * rcv_count,
         out_shape=[sd((4, 8, 128), F32)] * rcv_count,

time: 75.7 us -> 75.7 us (level)
  Pallas kernels: 16.2 us -> 17.2 us
  waiting for transfers between devices: 23.5 us -> 22.5 us
    pallas_call x1, Pallas kernels: 2.41 us -> 3.42 us  [local(): own(pltpu.with_memory_space_constraint(spec, pltpu.HBM), sketch.T)]
    ppermute x7, waiting for transfers between devices: 15.6 us -> 14.6 us  [local(): pieces[slot] = lax.ppermute(pieces[slot], 'rcv', pairs)]
  transfers between devices with their start and end apart: 12 -> 12, of which waited for: 7 -> 7; matrix products, arithmetic and copies ran while one was open for 0% -> 0% of each run, Pallas kernels for 4% -> 5%
where the time goes in v6:
time: 75.7 us; the launch traced here: 74.3 us
  starting transfers between devices  33.6 us (44%)
  waiting for transfers between devices  22.5 us (30%)
  Pallas kernels  17.2 us (23%)
    ppermute x7, starting transfers between devices, local(): pieces[slot] = lax.ppermute(pieces[slot], 'rcv', pairs)  17.4 us
    ppermute x7, waiting for transfers between devices, local(): pieces[slot] = lax.ppermute(pieces[slot], 'rcv', pairs)  14.6 us
    all_to_all x1, starting transfers between devices, local(): lax.all_to_all(spec.reshape(devices, 32, 128), ('src', 'rcv'), split_axis...  11.2 us
    pallas_call x1, Pallas kernels, local(): pl.pallas_call(dft_kernel, in_specs=[pl.BlockSpec(memory_space=pltpu.HBM)...  8.92 us
    ppermute x3, waiting for transfers between devices, local(): gram = gram + lax.ppermute(gram, 'src', [(s, s ^ bits) for s in range(src)])  6.24 us
    pallas_call x1, Pallas kernels, local(): own(pltpu.with_memory_space_constraint(spec, pltpu.HBM), sketch.T)  3.42 us
    pallas_call x1, Pallas kernels, local(): pl.pallas_call(lambda *refs: factor_kernel(scaling, *refs), out_shape=[sd...  3.24 us
    ppermute x1, starting transfers between devices, local(): other = lax.ppermute(gram, 'src', [(s, s ^ 7) for s in range(src)])  3.14 us
  transfers between devices with their start and end apart: 12, of which 7 were waited for; matrix products, arithmetic and copies ran while one was open for 0% of the time, Pallas kernels for 5%

profile of v6, /device:TPU:0, one launch (start us, length us, event | category | flops | bytes accessed | tf_op | source)
XLA Modules:
  0.0 74.3 jit_solution(15301893970596137157)
XLA Ops:
  0.6 8.9 %dft.1.spec_ref = f32[128,4,8,128]{3,2,1,0:T(8,128)} custom-call(f32[8,1024,512]{2,1,0:T(8,128)} %x_hbm.1, bf16[128,512]{1,0:T(8,128)(2,1)} %constant.2.clone.w_hbm), custom_call_target="tpu_custom_call" | custom-call | flops 1610612736 | bytes 19922944 | tf_op jit(solution)/shard_map/dft/pallas_call | solution.py:262
  9.6 0.0 copy-start
  9.6 11.2 %all-to-all-start = ((f32[128,32,128]{2,1,0:T(8,128)}), f32[128,32,128]{2,1,0:T(8,128)S(1)}, u32[]{:S(2)}, u32[]{:S(2)}) async-start(f32[128,32,128]{2,1,0:T(8,128)} %bitcast.5), calls=%async_computation | async-start | bytes 4194304 | tf_op jit(solution)/shard_map/all_to_all | solution.py:278
  20.8 0.0 copy-done
  20.8 3.4 %own.1 = (f32[4,8,128]{2,1,0:T(8,128)S(1)}, f32[4,8,128]{2,1,0:T(8,128)S(1)}, f32[4,8,128]{2,1,0:T(8,128)S(1)}, f32[4,8,128]{2,1,0:T(8,128)S(1)}, f32[4,8,128]{2...) custom-call(f32[128,4,8,128]{3,2,1,0:T(8,128)} %dft.1.spec_ref, ...), custom_call_target="tpu_custom_call" | custom-call | flops 3221225472 | bytes 4194304 | tf_op jit(solution)/shard_map/own/pallas_call | solution.py:296
  24.2 2.5 %collective-permute-start = (f32[4,8,128]{2,1,0:T(8,128)S(1)}, f32[4,8,128]{2,1,0:T(8,128)S(1)}, u32[]{:S(2)}, u32[]{:S(2)}) collective-permute-start(f32[4,8,128]{2,1,0:T(8,128)S(1)} %get-tuple-element.13), channel_id=1, source_target_pairs={{0,1},{1,0},{2,3},{3,2},{4,5},{5,4},{6,7},{7,6},{8,9},{9,8},{10,11... | collective-permute-start | bytes 49160 | tf_op jit(solution)/shard_map/ppermute | solution.py:299
  26.7 1.5 %collective-permute-start.1 = (f32[4,8,128]{2,1,0:T(8,128)S(1)}, f32[4,8,128]{2,1,0:T(8,128)S(1)}, u32[]{:S(2)}, u32[]{:S(2)}) collective-permute-start(f32[4,8,128]{2,1,0:T(8,128)S(1)} %get-tuple-element.14), channel_id=1, source_target_pairs={{0,2},{1,3},{2,0},{3,1},{4,6},{5,7},{6,4},{7,5},{8,10},{9,11},{10,... | collective-permute-start | bytes 49160 | tf_op jit(solution)/shard_map/ppermute | solution.py:299
  28.2 1.1 %collective-permute-start.2 = (f32[4,8,128]{2,1,0:T(8,128)S(1)}, f32[4,8,128]{2,1,0:T(8,128)S(1)}, u32[]{:S(2)}, u32[]{:S(2)}) collective-permute-start(f32[4,8,128]{2,1,0:T(8,128)S(1)} %get-tuple-element.15), channel_id=1, source_target_pairs={{0,3},{1,2},{2,1},{3,0},{4,7},{5,6},{6,5},{7,4},{8,11},{9,10},{10,... | collective-permute-start | bytes 49160 | tf_op jit(solution)/shard_map/ppermute | solution.py:299
  29.3 2.5 %collective-permute-start.3 = (f32[4,8,128]{2,1,0:T(8,128)S(1)}, f32[4,8,128]{2,1,0:T(8,128)S(1)}, u32[]{:S(2)}, u32[]{:S(2)}) collective-permute-start(f32[4,8,128]{2,1,0:T(8,128)S(1)} %get-tuple-element.16), channel_id=1, source_target_pairs={{0,4},{1,5},{2,6},{3,7},{4,0},{5,1},{6,2},{7,3},{8,12},{9,13},{10,... | collective-permute-start | bytes 49160 | tf_op jit(solution)/shard_map/ppermute | solution.py:299
  31.7 3.0 %collective-permute-start.4 = (f32[4,8,128]{2,1,0:T(8,128)S(1)}, f32[4,8,128]{2,1,0:T(8,128)S(1)}, u32[]{:S(2)}, u32[]{:S(2)}) collective-permute-start(f32[4,8,128]{2,1,0:T(8,128)S(1)} %get-tuple-element.17), channel_id=1, source_target_pairs={{0,5},{1,4},{2,7},{3,6},{4,1},{5,0},{6,3},{7,2},{8,13},{9,12},{10,... | collective-permute-start | bytes 49160 | tf_op jit(solution)/shard_map/ppermute | solution.py:299
  34.7 8.3 %collective-permute-done.refs_1_ = f32[4,8,128]{2,1,0:T(8,128)S(1)} collective-permute-done((f32[4,8,128]{2,1,0:T(8,128)S(1)}, f32[4,8,128]{2,1,0:T(8,128)S(1)}, u32[]{:S(2)}, u32[]{:S(2)}) %collective-permute-start) | collective-permute-done | bytes 16416 | tf_op jit(solution)/shard_map/ppermute | solution.py:299
  42.9 6.3 %collective-permute-start.5 = (f32[4,8,128]{2,1,0:T(8,128)S(1)}, f32[4,8,128]{2,1,0:T(8,128)S(1)}, u32[]{:S(2)}, u32[]{:S(2)}) collective-permute-start(f32[4,8,128]{2,1,0:T(8,128)S(1)} %get-tuple-element.18), channel_id=1, source_target_pairs={{0,6},{1,7},{2,4},{3,5},{4,2},{5,3},{6,0},{7,1},{8,14},{9,15},{10,... | collective-permute-start | bytes 49160 | tf_op jit(solution)/shard_map/ppermute | solution.py:299
  49.3 0.0 collective-permute-done.1.refs_2_
  49.3 0.6 collective-permute-start.6
  49.9 0.2 copy.5.s_ref
  50.1 0.2 prepare.1.s_ref
  50.3 0.0 collective-permute-done.2.refs_3_
  50.3 0.0 collective-permute-done.3.refs_4_
  50.3 0.0 collective-permute-done.4.refs_5_
  50.3 0.7 collective-permute-done.5.refs_6_
  51.0 5.6 %collective-permute-done.6.refs_7_ = f32[4,8,128]{2,1,0:T(8,128)S(1)} collective-permute-done((f32[4,8,128]{2,1,0:T(8,128)S(1)}, f32[4,8,128]{2,1,0:T(8,128)S(1)}, u32[]{:S(2)}, u32[]{:S(2)}) %collective-permute-start.6) | collective-permute-done | bytes 16416 | tf_op jit(solution)/shard_map/ppermute | solution.py:299
  56.6 0.1 place.1.d_ref
  56.8 0.0 all-to-all-done
  56.8 1.3 %sketch.1 = (f32[72,128]{1,0:T(8,128)S(1)}, f32[2,128,128]{2,1,0:T(8,128)S(1)}) custom-call(f32[4096,128]{1,0:T(8,128)S(1)} %bitcast.3, f32[2,128,128]{2,1,0:T(8,128)S(1)} %place.1.d_ref, bf16[256,512]{1,0:T(8,128)(2,1)S(1)} %prepare.1.s_ref), custom_call_target="tpu_custom_call" | custom-call | tf_op jit(solution)/shard_map/sketch/pallas_call | solution.py:301
  58.1 0.1 collective-permute-start.7
  58.2 1.2 %collective-permute-done.7 = f32[72,128]{1,0:T(8,128)S(1)} collective-permute-done((f32[72,128]{1,0:T(8,128)S(1)}, f32[72,128]{1,0:T(8,128)S(1)}, u32[]{:S(2)}, u32[]{:S(2)}) %collective-permute-start.7) | collective-permute-done | bytes 36896 | tf_op jit(solution)/shard_map/ppermute | solution.py:310
  59.4 0.4 collective-permute-start.8
  59.7 3.1 %collective-permute-done.8 = f32[72,128]{1,0:T(8,128)S(1)} collective-permute-done((f32[72,128]{1,0:T(8,128)S(1)}, f32[72,128]{1,0:T(8,128)S(1)}, u32[]{:S(2)}, u32[]{:S(2)}) %collective-permute-start.8) | collective-permute-done | bytes 36896 | tf_op jit(solution)/shard_map/ppermute | solution.py:310
  62.8 1.5 %collective-permute-start.9 = (f32[72,128]{1,0:T(8,128)S(1)}, f32[72,128]{1,0:T(8,128)S(1)}, u32[]{:S(2)}, u32[]{:S(2)}) collective-permute-start(f32[72,128]{1,0:T(8,128)S(1)} %add.10), channel_id=1, source_target_pairs={{0,24},{8,16},{16,8},{24,0},{32,56},{40,48},{48,40},{56,32},{64,88... | collective-permute-start | bytes 110600 | tf_op jit(solution)/shard_map/ppermute | solution.py:310
  64.3 2.0 %collective-permute-done.9 = f32[72,128]{1,0:T(8,128)S(1)} collective-permute-done((f32[72,128]{1,0:T(8,128)S(1)}, f32[72,128]{1,0:T(8,128)S(1)}, u32[]{:S(2)}, u32[]{:S(2)}) %collective-permute-start.9) | collective-permute-done | bytes 36896 | tf_op jit(solution)/shard_map/ppermute | solution.py:310
  66.3 3.1 %collective-permute-start.10 = (f32[72,128]{1,0:T(8,128)S(1)}, f32[72,128]{1,0:T(8,128)S(1)}, u32[]{:S(2)}, u32[]{:S(2)}) collective-permute-start(f32[72,128]{1,0:T(8,128)S(1)} %add.11.refs_0_), channel_id=1, source_target_pairs={{0,56},{8,48},{16,40},{24,32},{32,24},{40,16},{48,8},{56,0},{64,12... | collective-permute-start | bytes 110600 | tf_op jit(solution)/shard_map/ppermute | solution.py:311
  69.4 1.6 %collective-permute-done.10.refs_1_ = f32[72,128]{1,0:T(8,128)S(1)} collective-permute-done((f32[72,128]{1,0:T(8,128)S(1)}, f32[72,128]{1,0:T(8,128)S(1)}, u32[]{:S(2)}, u32[]{:S(2)}) %collective-permute-start.10) | collective-permute-done | bytes 36896 | tf_op jit(solution)/shard_map/ppermute | solution.py:311
  71.0 3.2 %factor.1 = (f32[4,2,64,64]{3,2,1,0:T(8,128)}, f32[4,64,64]{2,1,0:T(8,128)}) custom-call(f32[72,128]{1,0:T(8,128)S(1)} %add.11.refs_0_, f32[72,128]{1,0:T(8,128)S(1)} %collective-permute-done.10.refs_1_, f32[2,128,128]{2,1,0:T(8,128)S(1)} %get-tuple-element.21.refs_2_), custom_call_target="tpu_custom_call" | custom-call | tf_op jit(solution)/shard_map/factor/pallas_call | solution.py:313
  (3 shorter events, 0.0 us)
Async XLA Ops:
  9.6 11.2 %copy-start = (f32[1024,64]{0,1:T(8,128)S(1)}, f32[1024,64]{0,1:T(8,128)}, u32[]{:S(2)}) copy-start(f32[1024,64]{0,1:T(8,128)} %param.4) | copy-start | bytes 786436
  9.6 47.2 %all-to-all-start = ((f32[128,32,128]{2,1,0:T(8,128)}), f32[128,32,128]{2,1,0:T(8,128)S(1)}, u32[]{:S(2)}, u32[]{:S(2)}) async-start(f32[128,32,128]{2,1,0:T(8,128)} %bitcast.5), calls=%async_computation | async-start | bytes 4194304 | tf_op jit(solution)/shard_map/all_to_all | solution.py:278
  24.2 18.8 %collective-permute-start = (f32[4,8,128]{2,1,0:T(8,128)S(1)}, f32[4,8,128]{2,1,0:T(8,128)S(1)}, u32[]{:S(2)}, u32[]{:S(2)}) collective-permute-start(f32[4,8,128]{2,1,0:T(8,128)S(1)} %get-tuple-element.13), channel_id=1, source_target_pairs={{0,1},{1,0},{2,3},{3,2},{4,5},{5,4},{6,7},{7,6},{8,9},{9,8},{10,11... | collective-permute-start | bytes 49160 | tf_op jit(solution)/shard_map/ppermute | solution.py:299
  26.7 22.5 %collective-permute-start.1 = (f32[4,8,128]{2,1,0:T(8,128)S(1)}, f32[4,8,128]{2,1,0:T(8,128)S(1)}, u32[]{:S(2)}, u32[]{:S(2)}) collective-permute-start(f32[4,8,128]{2,1,0:T(8,128)S(1)} %get-tuple-element.14), channel_id=1, source_target_pairs={{0,2},{1,3},{2,0},{3,1},{4,6},{5,7},{6,4},{7,5},{8,10},{9,11},{10,... | collective-permute-start | bytes 49160 | tf_op jit(solution)/shard_map/ppermute | solution.py:299
  28.2 22.1 %collective-permute-start.2 = (f32[4,8,128]{2,1,0:T(8,128)S(1)}, f32[4,8,128]{2,1,0:T(8,128)S(1)}, u32[]{:S(2)}, u32[]{:S(2)}) collective-permute-start(f32[4,8,128]{2,1,0:T(8,128)S(1)} %get-tuple-element.15), channel_id=1, source_target_pairs={{0,3},{1,2},{2,1},{3,0},{4,7},{5,6},{6,5},{7,4},{8,11},{9,10},{10,... | collective-permute-start | bytes 49160 | tf_op jit(solution)/shard_map/ppermute | solution.py:299
  29.3 21.0 %collective-permute-start.3 = (f32[4,8,128]{2,1,0:T(8,128)S(1)}, f32[4,8,128]{2,1,0:T(8,128)S(1)}, u32[]{:S(2)}, u32[]{:S(2)}) collective-permute-start(f32[4,8,128]{2,1,0:T(8,128)S(1)} %get-tuple-element.16), channel_id=1, source_target_pairs={{0,4},{1,5},{2,6},{3,7},{4,0},{5,1},{6,2},{7,3},{8,12},{9,13},{10,... | collective-permute-start | bytes 49160 | tf_op jit(solution)/shard_map/ppermute | solution.py:299
  31.7 18.6 %collective-permute-start.4 = (f32[4,8,128]{2,1,0:T(8,128)S(1)}, f32[4,8,128]{2,1,0:T(8,128)S(1)}, u32[]{:S(2)}, u32[]{:S(2)}) collective-permute-start(f32[4,8,128]{2,1,0:T(8,128)S(1)} %get-tuple-element.17), channel_id=1, source_target_pairs={{0,5},{1,4},{2,7},{3,6},{4,1},{5,0},{6,3},{7,2},{8,13},{9,12},{10,... | collective-permute-start | bytes 49160 | tf_op jit(solution)/shard_map/ppermute | solution.py:299
  42.9 8.0 %collective-permute-start.5 = (f32[4,8,128]{2,1,0:T(8,128)S(1)}, f32[4,8,128]{2,1,0:T(8,128)S(1)}, u32[]{:S(2)}, u32[]{:S(2)}) collective-permute-start(f32[4,8,128]{2,1,0:T(8,128)S(1)} %get-tuple-element.18), channel_id=1, source_target_pairs={{0,6},{1,7},{2,4},{3,5},{4,2},{5,3},{6,0},{7,1},{8,14},{9,15},{10,... | collective-permute-start | bytes 49160 | tf_op jit(solution)/shard_map/ppermute | solution.py:299
  49.3 7.4 %collective-permute-start.6 = (f32[4,8,128]{2,1,0:T(8,128)S(1)}, f32[4,8,128]{2,1,0:T(8,128)S(1)}, u32[]{:S(2)}, u32[]{:S(2)}) collective-permute-start(f32[4,8,128]{2,1,0:T(8,128)S(1)} %get-tuple-element.19), channel_id=1, source_target_pairs={{0,7},{1,6},{2,5},{3,4},{4,3},{5,2},{6,1},{7,0},{8,15},{9,14},{10,... | collective-permute-start | bytes 49160 | tf_op jit(solution)/shard_map/ppermute | solution.py:299
  58.1 1.3 %collective-permute-start.7 = (f32[72,128]{1,0:T(8,128)S(1)}, f32[72,128]{1,0:T(8,128)S(1)}, u32[]{:S(2)}, u32[]{:S(2)}) collective-permute-start(f32[72,128]{1,0:T(8,128)S(1)} %get-tuple-element.20), channel_id=1, source_target_pairs={{0,8},{8,0},{16,24},{24,16},{32,40},{40,32},{48,56},{56,48},{64,72... | collective-permute-start | bytes 110600 | tf_op jit(solution)/shard_map/ppermute | solution.py:310
  59.4 3.4 %collective-permute-start.8 = (f32[72,128]{1,0:T(8,128)S(1)}, f32[72,128]{1,0:T(8,128)S(1)}, u32[]{:S(2)}, u32[]{:S(2)}) collective-permute-start(f32[72,128]{1,0:T(8,128)S(1)} %add.9), channel_id=1, source_target_pairs={{0,72},{8,64},{16,88},{24,80},{32,104},{40,96},{48,120},{56,112},{... | collective-permute-start | bytes 110600 | tf_op jit(solution)/shard_map/ppermute | solution.py:310
  62.8 3.4 %collective-permute-start.9 = (f32[72,128]{1,0:T(8,128)S(1)}, f32[72,128]{1,0:T(8,128)S(1)}, u32[]{:S(2)}, u32[]{:S(2)}) collective-permute-start(f32[72,128]{1,0:T(8,128)S(1)} %add.10), channel_id=1, source_target_pairs={{0,24},{8,16},{16,8},{24,0},{32,56},{40,48},{48,40},{56,32},{64,88... | collective-permute-start | bytes 110600 | tf_op jit(solution)/shard_map/ppermute | solution.py:310
  66.3 4.8 %collective-permute-start.10 = (f32[72,128]{1,0:T(8,128)S(1)}, f32[72,128]{1,0:T(8,128)S(1)}, u32[]{:S(2)}, u32[]{:S(2)}) collective-permute-start(f32[72,128]{1,0:T(8,128)S(1)} %add.11.refs_0_), channel_id=1, source_target_pairs={{0,56},{8,48},{16,40},{24,32},{32,24},{40,16},{48,8},{56,0},{64,12... | collective-permute-start | bytes 110600 | tf_op jit(solution)/shard_map/ppermute | solution.py:311
